TPU v7x, 128 devices: a whole 4x4x4 slice. The times are simulated.
128 devices in a mesh: dp: 4 (over x), clus: 32 (over y, z, core).
Axes of the slice: x: 4, y: 4, z: 4, core: 2. Of those that a mesh axis runs over, the one named last changes fastest.
Arguments:
- embeddings: bfloat16 [65536, 1024], P(('dp', 'clus')), may hold values from -8 to 8
- parents: int32 [65536, 8], P(('dp', 'clus')), may hold values from 0 to 255, all different within a row; in each aligned block of 512 rows (0 to 511, 512 to 1023, ...) at most 32 rows name the same one
- children: int32 [65536, 8], P(('dp', 'clus')), may hold values from 0 to 1
- temper: float32 [256], P('clus'), may hold values from 0.5 to 2
- level_two: bfloat16 [32768, 1024], P('clus'), may hold values from -2 to 2
- level_three: bfloat16 [65536, 1024], P('clus'), may hold values from -0.1875 to 0.1875
Outputs:
- soft_codes: bfloat16 [65536, 1024], P(('dp', 'clus'))
- candidate_scores: float32 [65536, 1024], P(('dp', 'clus'))
- new_centroids: float32 [32768, 1024], P('clus')
- cluster_mass: float32 [32768], P('clus')
Inputs may be any that keep to these rules, and one draw needn't show every extreme that they name: `parents`: each row names 8 different blocks. Among the rows of one device no block is named by more than 32 rows, and in every draw some block is named by exactly 32 rows of one device.
All inputs are finite; a program needn't handle non-finite values.
Results may differ from a plain program's by a relative error of at most 0.0045.
Values may be sent and summed in bfloat16 or wider, within the bound.
A program may use at most 192 MiB of HBM per device.

v0:
```python
import math

import jax
import jax.numpy as jnp
from jax import lax
from jax.sharding import PartitionSpec as P


def local_ranks(block_ids, first_block, block_count):
    length = block_ids.shape[-1]
    group = math.gcd(length, 128)
    groups = length // group
    leading = block_ids.shape[:-1]
    onehot = (
        (block_ids - first_block)[..., None] == jnp.arange(block_count, dtype=jnp.int32)
    ).astype(jnp.bfloat16)
    grouped = onehot.reshape(leading + (groups, group, block_count))
    lower = (jnp.arange(group)[:, None] > jnp.arange(group)[None, :]).astype(jnp.bfloat16)
    within = jnp.einsum("ij,...gjb->...gib", lower, grouped, preferred_element_type=jnp.float32)
    group_sums = jnp.sum(grouped, axis=-2, dtype=jnp.float32)
    earlier = (jnp.arange(groups)[:, None] > jnp.arange(groups)[None, :]).astype(jnp.float32)
    before = jnp.einsum("hg,...gb->...hb", earlier, group_sums, precision=lax.Precision.HIGHEST)
    counted = within + before[..., None, :]
    position = jnp.sum(counted * grouped.astype(jnp.float32), axis=-1).reshape(leading + (length,))
    return (onehot, position)


def slot_table(onehot, position, most_rows):
    length = position.shape[-1]
    rank_hot = (position[..., None] == jnp.arange(most_rows, dtype=jnp.float32)).astype(jnp.float32)
    numbers = jnp.arange(length, dtype=jnp.float32) + 1.0
    located = jnp.einsum(
        "...nb,...nk->...bk",
        onehot.astype(jnp.float32),
        rank_hot * numbers[:, None],
        precision=lax.Precision.HIGHEST,
    )
    located = located.reshape(located.shape[:-2] + (located.shape[-2] * located.shape[-1],))
    return (located + 0.5).astype(jnp.int32) - 1


def body(embeddings, parents, children, temper, level_two, level_three):
    row_count, features = embeddings.shape
    parent_count = parents.shape[1]
    blocks_here = temper.shape[0]
    block_size = level_two.shape[0] // blocks_here
    child_count = level_three.shape[0] // (blocks_here * block_size)
    shard_count = lax.axis_size("clus")
    own_index = lax.axis_index("clus")
    all_blocks = blocks_here * shard_count
    most_rows = 2 * row_count * parent_count // all_blocks
    item_count = row_count * parent_count
    slot_count = blocks_here * most_rows
    flat_blocks = parents.reshape(item_count)
    own_onehot, own_position = local_ranks(flat_blocks, 0, all_blocks)
    global_slot = flat_blocks * most_rows + own_position.astype(jnp.int32)
    own_item = slot_table(own_onehot, own_position, most_rows)
    own_filled = own_item >= 0
    own_safe = jnp.maximum(own_item, 0)
    all_rows, all_parents, all_children = (
        lax.all_gather(embeddings, "clus", axis=0, tiled=True),
        lax.all_gather(parents, "clus", axis=0, tiled=True),
        lax.all_gather(children, "clus", axis=0, tiled=True),
    )
    source_blocks = all_parents.reshape(shard_count, item_count)
    mine_onehot, mine_position = local_ranks(source_blocks, own_index * blocks_here, blocks_here)
    local_table = slot_table(mine_onehot, mine_position, most_rows)
    sources = jnp.arange(shard_count, dtype=jnp.int32)[:, None]
    slot_item = jnp.where(local_table >= 0, sources * item_count + local_table, -1).reshape(-1)
    filled = slot_item >= 0
    safe_item = jnp.maximum(slot_item, 0)
    slot_rows = jnp.where(filled[:, None], jnp.take(all_rows, safe_item // parent_count, axis=0), 0)
    slot_child = jnp.where(filled, all_children.reshape(-1)[safe_item], -1)
    slot_rows = slot_rows.reshape(shard_count, blocks_here, most_rows, features)
    slot_child = slot_child.reshape(shard_count, blocks_here, most_rows)
    centroids = level_two.reshape(blocks_here, block_size, features)
    scores = jnp.einsum("sbmd,bcd->sbmc", slot_rows, centroids, preferred_element_type=jnp.float32)
    scores = scores * temper[None, :, None, None]
    third = level_three.reshape(blocks_here, child_count, block_size, features)
    deeper = jnp.zeros(scores.shape, jnp.float32)
    for child in range(child_count):
        product = jnp.einsum(
            "sbmd,bcd->sbmc", slot_rows, third[:, child], preferred_element_type=jnp.float32
        )
        deeper = jnp.where((slot_child == child)[..., None], product, deeper)
    back_scores, back_deeper = (
        lax.all_to_all(scores, "clus", split_axis=0, concat_axis=0, tiled=True),
        lax.all_to_all(deeper, "clus", split_axis=0, concat_axis=0, tiled=True),
    )
    item_scores = back_scores.reshape(all_blocks * most_rows, block_size)[global_slot].reshape(
        row_count, parent_count * block_size
    )
    item_deeper = back_deeper.reshape(all_blocks * most_rows, block_size)[global_slot].reshape(
        row_count, parent_count, block_size
    )
    top = jnp.max(item_scores, axis=1, keepdims=True)
    weights = jnp.exp(item_scores - top)
    total = jnp.sum(weights, axis=1, keepdims=True)
    probs = weights / total
    soft_codes = probs.astype(jnp.bfloat16)
    mass = probs.reshape(row_count, parent_count, block_size).sum(axis=2)
    candidate_scores = (parent_count * mass[:, :, None] * item_deeper).reshape(
        row_count, parent_count * block_size
    )
    code_items = probs.reshape(item_count, block_size)
    send_codes = jnp.where(own_filled[:, None], code_items[own_safe], 0.0)
    owner_codes = lax.all_to_all(
        send_codes.reshape(shard_count, slot_count, block_size),
        "clus",
        split_axis=0,
        concat_axis=0,
        tiled=True,
    )
    owner_codes = owner_codes.reshape(shard_count, blocks_here, most_rows, block_size)
    code_high = owner_codes.astype(jnp.bfloat16)
    code_low = (owner_codes - code_high.astype(jnp.float32)).astype(jnp.bfloat16)
    code_pair = jnp.concatenate([code_high, code_low], axis=-1)
    pair_sums = jnp.einsum(
        "sbmc,sbmd->bcd", code_pair, slot_rows, preferred_element_type=jnp.float32
    )
    partial_sums = pair_sums[:, :block_size] + pair_sums[:, block_size:]
    partial_mass = jnp.sum(owner_codes, axis=(0, 2))
    weighted, cluster_mass = lax.psum((partial_sums, partial_mass), "dp")
    cluster_mass = cluster_mass.reshape(blocks_here * block_size)
    new_centroids = (
        weighted.reshape(blocks_here * block_size, features)
        / jnp.maximum(cluster_mass, 1.0)[:, None]
    )
    return (soft_codes, candidate_scores, new_centroids, cluster_mass)


def solution(mesh):
    in_specs = (
        P(("dp", "clus"), None),
        P(("dp", "clus"), None),
        P(("dp", "clus"), None),
        P("clus"),
        P("clus", None),
        P("clus", None),
    )
    out_specs = (P(("dp", "clus"), None), P(("dp", "clus"), None), P("clus", None), P("clus"))
    return jax.shard_map(body, mesh=mesh, in_specs=in_specs, out_specs=out_specs, check_vma=False)
```

profile of v0, /device:TPU:8, one launch (start us, length us, event | category | flops | bytes accessed | tf_op | source)
XLA Modules:
  0.0 807.3 jit_solution(16947258658350363316)
XLA Ops:
  7.9 26.7 %all_gather.9 = s32[16384,8]{0,1:T(8,128)S(1)} all-gather(s32[512,8]{0,1:T(8,128)} %param.7), channel_id=1, replica_groups=mesh['dp'=4,'clus'=32] {'clus'}, dimensions={0}, use_global_device_ids=true | all-gather | bytes 540672 | tf_op jit(solution)/shard_map/all_gather | solution.py:62
  34.7 5.2 copy.63
  39.9 6.4 sub.61
  46.3 7.6 sub.60
  59.0 9.0 %fusion.34 = s32[32,8,32]{2,1,0:T(8,128)S(1)} fusion(f32[4096]{0:T(1024)S(1)} %iota_add_fusion, f32[32,4096]{1,0:T(8,128)S(1)} %bitcast.88, s32[32,4096]{1,0:T(8,128)S(1)} %copy-done.5), kind=kOutput, calls=%fused_computation.55 | convolution fusion | flops 412114944 | bytes 1097728 | tf_op jit(solution)/shard_map/...nb,...nk->...bk/dot_general | solution.py:32
  68.2 24.0 %all_gather.11 = s32[16384,8]{0,1:T(8,128)S(1)} all-gather(s32[512,8]{0,1:T(8,128)S(1)} %copy-done.7), channel_id=1, replica_groups=mesh['dp'=4,'clus'=32] {'clus'}, dimensions={0}, use_global_device_ids=true | all-gather | bytes 540672 | tf_op jit(solution)/shard_map/all_gather | solution.py:63
  92.3 5.4 copy.73
  97.6 6.7 reshape.338
  104.5 45.5 %gather_fusion.2 = s32[8192]{0:T(1024)S(1)} fusion(s32[131072]{0:T(1024)S(1)} %reshape.338, s32[8192]{0:T(1024)S(1)} %broadcast_clamp_fusion.1), kind=kCustom, calls=%fused_computation.2 | custom fusion | bytes 98304 | tf_op jit(solution)/shard_map/gather | solution.py:73
  150.7 271.9 %gather_fusion = bf16[8192,1024]{1,0:T(8,128)(2,1)} fusion(bf16[16384,1024]{1,0:T(8,128)(2,1)} %all-gather.2.cloned.1.call-done, s32[8192]{0:T(1024)S(1)} %broadcast_clamp_fusion.2), kind=kCustom, calls=%fused_computation | custom fusion | bytes 33587200 | tf_op jit(solution)/shard_map/jit(_take)/gather | solution.py:72
  422.6 21.6 %multiply_bitcast_fusion = f32[32,8,32,128]{3,0,2,1:T(8,128)S(1)} fusion(f32[8]{0:T(128)S(1)} %copy-done.10, bf16[8,128,1024,1]{2,1,3,0:T(8,128)(2,1)S(1)} %bitcast.79, bf16[32,8,32,1024]{3,2,1,0:T(8,128)(2,1)} %bitcast.80, pred[32,8,32]{0,2,1:T(8,128)(4,1)S(1)} %copy.68, pred[32,8,32]{0,2,1:T(8,128)(4,1)S(1)} %copy.67), kind=kOutput, calls=%fused_computation.31 | convolution fusion | flops 2165309440 | bytes 23085088 | tf_op jit(solution)/shard_map/sbmd,bcd->sbmc/dot_general | solution.py:77
  444.2 4.4 copy.70
  448.7 53.0 %all-to-all-start = ((f32[32,8,32,128]{3,2,1,0:T(8,128)}), f32[32,8,32,128]{3,2,1,0:T(8,128)}, u32[]{:S(2)}, u32[]{:S(2)}) async-start(f32[32,8,32,128]{3,2,1,0:T(8,128)} %copy.70), calls=%async_computation | async-start | bytes 8388608 | tf_op jit(solution)/shard_map/all_to_all | solution.py:87
  507.3 44.1 %all-to-all-done = f32[32,8,32,128]{3,2,1,0:T(8,128)} async-done(((f32[32,8,32,128]{3,2,1,0:T(8,128)}), f32[32,8,32,128]{3,2,1,0:T(8,128)}, u32[]{:S(2)}, u32[]{:S(2)}) %all-to-all-start) | async-done | bytes 4194336 | tf_op jit(solution)/shard_map/all_to_all | solution.py:87
  551.4 12.9 %gather_fusion.1 = f32[4096,128]{1,0:T(8,128)S(1)} fusion(f32[8192,128]{1,0:T(8,128)} %bitcast.11, s32[4096]{0:T(1024)S(1)} %broadcast_clamp_fusion.3), kind=kCustom, calls=%fused_computation.1 | custom fusion | bytes 4210688 | tf_op jit(solution)/shard_map/gather | solution.py:90
  567.5 3.1 fusion.61
  570.6 28.0 %gather_fusion.4 = f32[8192,128]{1,0:T(8,128)} fusion(f32[4096,128]{1,0:T(8,128)S(1)} %get-tuple-element.7, s32[8192]{0:T(1024)S(1)} %broadcast_clamp_fusion), kind=kCustom, calls=%fused_computation.4 | custom fusion | bytes 8421376 | tf_op jit(solution)/shard_map/gather | solution.py:106
  598.5 5.2 broadcast_select_fusion
  603.8 9.7 %all-to-all-start.2 = ((f32[32,256,128]{2,1,0:T(8,128)}), f32[32,256,128]{2,1,0:T(8,128)}, u32[]{:S(2)}, u32[]{:S(2)}) async-start(f32[32,256,128]{2,1,0:T(8,128)} %broadcast_select_fusion), calls=%async_computation.2 | async-start | bytes 8388608 | tf_op jit(solution)/shard_map/all_to_all | solution.py:107
  613.5 21.8 %fusion.21 = f32[8,32,32,128]{3,1,2,0:T(8,128)S(1)} fusion(bf16[8,2,128,1024]{3,2,1,0:T(8,128)(2,1)} %bitcast.97, bf16[32,8,32,1024]{3,2,1,0:T(8,128)(2,1)} %bitcast.81, pred[32,8,32]{0,2,1:T(8,128)(4,1)S(1)} %copy.68, pred[32,8,32]{0,2,1:T(8,128)(4,1)S(1)} %copy.67), kind=kOutput, calls=%fused_computation.41 | convolution fusion | flops 2164260864 | bytes 23085056 | tf_op jit(solution)/shard_map/sbmd,bcd->sbmc/dot_general | solution.py:82
  635.3 17.8 %fusion.12 = f32[32,8,32,128]{3,0,2,1:T(8,128)S(1)} fusion(f32[8,32,32,128]{3,1,2,0:T(8,128)S(1)} %fusion.21, bf16[8,2,128,1024]{3,2,1,0:T(8,128)(2,1)S(1)} %bitcast.98, pred[32,8,32]{0,2,1:T(8,128)(4,1)S(1)} %copy.76, pred[32,8,32]{0,2,1:T(8,128)(4,1)S(1)} %copy.74, bf16[32,8,32,1024]{3,2,1,0:T(8,128)(2,1)} %bitcast.82, pred[32,8,32]{0,2,1:T(8,128)(4,1)S(1)} %copy.68, ...), kind=kOutput, calls=%fused_computation.25 | convolution fusion | flops 2166358016 | bytes 27394048 | tf_op jit(solution)/shard_map/sbmd,bcd->sbmc/dot_general | solution.py:82
  653.1 4.4 copy.78
  657.5 5.7 all-to-all-done.2
  663.2 9.2 %all-to-all-start.1 = ((f32[32,8,32,128]{3,2,1,0:T(8,128)}), f32[32,8,32,128]{3,2,1,0:T(8,128)}, u32[]{:S(2)}, u32[]{:S(2)}) async-start(f32[32,8,32,128]{3,2,1,0:T(8,128)} %copy.78), calls=%async_computation.1 | async-start | bytes 8388608 | tf_op jit(solution)/shard_map/all_to_all | solution.py:88
  672.5 4.6 copy.82
  677.9 22.2 %fusion.18 = f32[8,256,1024]{2,1,0:T(8,128)S(1)} fusion(bf16[32,8,32,128]{3,0,2,1:T(8,128)(2,1)S(1)} %get-tuple-element.4, bf16[32,8,32,128]{3,0,2,1:T(8,128)(2,1)S(1)} %get-tuple-element.5, bf16[32,8,32,1024]{3,2,1,0:T(8,128)(2,1)} %bitcast.83, pred[32,8,32]{0,2,1:T(8,128)(4,1)S(1)} %copy.68, pred[32,8,32]{0,2,1:T(8,128)(4,1)S(1)} %copy.67), kind=kOutput, calls=%fused_computation.37 | convolution fusion | flops 4320133120 | bytes 29376512 | tf_op jit(solution)/shard_map/sbmc,sbmd->bcd/dot_general | solution.py:118
  706.1 16.3 %all-to-all-done.1 = f32[32,8,32,128]{3,2,1,0:T(8,128)} async-done(((f32[32,8,32,128]{3,2,1,0:T(8,128)}), f32[32,8,32,128]{3,2,1,0:T(8,128)}, u32[]{:S(2)}, u32[]{:S(2)}) %all-to-all-start.1) | async-done | bytes 4194336 | tf_op jit(solution)/shard_map/all_to_all | solution.py:88
  722.4 16.5 %gather_fusion.3 = f32[4096,128]{1,0:T(8,128)} fusion(f32[8192,128]{1,0:T(8,128)} %bitcast.26, s32[4096]{0:T(1024)S(1)} %broadcast_clamp_fusion.3), kind=kCustom, calls=%fused_computation.3 | custom fusion | bytes 4210688 | tf_op jit(solution)/shard_map/gather | solution.py:93
  742.5 4.4 bitcast_multiply_fusion
  749.4 9.1 %psum.15 = f32[1024]{0:T(1024)S(1)} all-reduce(f32[1024]{0:T(1024)S(1)} %bitcast.95), channel_id=1, replica_groups=mesh['dp'=4,'clus'=32] {'dp'}, use_global_device_ids=true, to_apply=%region_12.13 | all-reduce | flops 1024 | bytes 8192 | tf_op jit(solution)/shard_map/psum | solution.py:123
  758.5 36.8 %all-reduce.2.cloned.1.call-done = f32[1024,1024]{1,0:T(8,128)} async-done(((f32[1024,1024]{1,0:T(8,128)}), f32[1024,1024]{1,0:T(8,128)}) %all-reduce.2.cloned.1.call-update) | async-done | bytes 4194320 | tf_op jit(solution)/shard_map/psum | solution.py:123
  795.3 4.7 broadcast_divide_fusion
  (88 shorter events, 28.2 us)
Async XLA Ops:
  7.2 415.4 %copy-start = (bf16[1024,1024]{1,0:T(8,128)(2,1)S(1)}, bf16[1024,1024]{1,0:T(8,128)(2,1)}, u32[]{:S(2)}) copy-start(bf16[1024,1024]{1,0:T(8,128)(2,1)} %param.10) | copy-start | bytes 6291460
  7.2 143.5 %all-gather.2.cloned.1.call-start = ((), (), s32[]{:S(2)}) async-start(), calls=%async_computation.3 | async-start | bytes 34603008 | tf_op jit(solution)/shard_map/all_gather | solution.py:61
  55.8 3.2 copy-start.5
  59.0 9.2 %copy-start.7 = (s32[512,8]{0,1:T(8,128)S(1)}, s32[512,8]{0,1:T(8,128)}, u32[]{:S(2)}) copy-start(s32[512,8]{0,1:T(8,128)} %param.8) | copy-start | bytes 49156
  150.6 272.0 %copy-start.10 = (f32[8]{0:T(128)S(1)}, f32[8]{0:T(128)}, u32[]{:S(2)}) copy-start(f32[8]{0:T(128)} %param.9) | copy-start | bytes 100
  448.7 53.0 %copy-start.6 = (s32[512,8]{0,1:T(8,128)S(1)}, s32[512,8]{0,1:T(8,128)}, u32[]{:S(2)}) copy-start(s32[512,8]{0,1:T(8,128)} %param.7) | copy-start | bytes 49156
  448.7 102.7 %all-to-all-start = ((f32[32,8,32,128]{3,2,1,0:T(8,128)}), f32[32,8,32,128]{3,2,1,0:T(8,128)}, u32[]{:S(2)}, u32[]{:S(2)}) async-start(f32[32,8,32,128]{3,2,1,0:T(8,128)} %copy.70), calls=%async_computation | async-start | bytes 8388608 | tf_op jit(solution)/shard_map/all_to_all | solution.py:87
  564.4 3.0 copy-start.2
  603.8 59.4 %all-to-all-start.2 = ((f32[32,256,128]{2,1,0:T(8,128)}), f32[32,256,128]{2,1,0:T(8,128)}, u32[]{:S(2)}, u32[]{:S(2)}) async-start(f32[32,256,128]{2,1,0:T(8,128)} %broadcast_select_fusion), calls=%async_computation.2 | async-start | bytes 8388608 | tf_op jit(solution)/shard_map/all_to_all | solution.py:107
  613.5 21.8 %copy-start.9 = (bf16[2048,1024]{1,0:T(8,128)(2,1)S(1)}, bf16[2048,1024]{1,0:T(8,128)(2,1)}, u32[]{:S(2)}) copy-start(bf16[2048,1024]{1,0:T(8,128)(2,1)} %param.11) | copy-start | bytes 12582916
  663.2 59.2 %all-to-all-start.1 = ((f32[32,8,32,128]{3,2,1,0:T(8,128)}), f32[32,8,32,128]{3,2,1,0:T(8,128)}, u32[]{:S(2)}, u32[]{:S(2)}) async-start(f32[32,8,32,128]{3,2,1,0:T(8,128)} %copy.78), calls=%async_computation.1 | async-start | bytes 8388608 | tf_op jit(solution)/shard_map/all_to_all | solution.py:88
  672.5 122.8 %all-reduce.2.cloned.1.call-start = ((), (), s32[]{:S(2)}) async-start(), calls=%async_computation.4 | async-start | bytes 8388608 | tf_op jit(solution)/shard_map/psum | solution.py:123
  703.0 1.6 copy-start.3
  738.9 3.6 copy-start.4
  758.5 41.5 %copy-start.8 = (f32[1024]{0:T(1024)}, f32[1024]{0:T(1024)S(1)}, u32[]{:S(2)}) copy-start(f32[1024]{0:T(1024)S(1)} %psum.15) | copy-start | bytes 12292
  758.5 41.5 %copy-start.1 = (bf16[1024,1024]{1,0:T(8,128)(2,1)S(1)}, bf16[1024,1024]{1,0:T(8,128)(2,1)}, u32[]{:S(2)}) copy-start(bf16[1024,1024]{1,0:T(8,128)(2,1)} %param.10) | copy-start | bytes 6291460
Sparse Core Ops, SparseCore 0:
  10.3 117.9 all-gather.1
  703.2 92.0 all-reduce.1
where the time goes:
time: 820 us; the launch traced here: 807 us
  local copies, waits for them, and re-layouts  430 us (52%)
  waiting for transfers between devices  104 us (13%)
  matrix products  98.9 us (12%)
  starting transfers between devices  72 us (9%)
  blocking collectives  59.8 us (7%)
  other arithmetic  28.1 us (3%)
  between operations  15.1 us (2%)
    gather x1, local copies, waits for them, and re-layouts, body(): jnp.take(all_rows, safe_item // parent_count, axis=0)  272 us
    all_to_all x1, starting transfers between devices, body(): lax.all_to_all(scores, 'clus', split_axis=0, concat_axis=0, tiled=True)  53 us
    gather x2, local copies, waits for them, and re-layouts, body(): slot_child = jnp.where(filled, all_children.reshape(-1)[safe_item], -1)  45.6 us
    all_to_all x1, waiting for transfers between devices, body(): lax.all_to_all(scores, 'clus', split_axis=0, concat_axis=0, tiled=True)  44.1 us
    dot_general x2, matrix products, body(): jnp.einsum('sbmd,bcd->sbmc', slot_rows, third[:, child], preferred_elemen...  39.6 us
    psum x1, waiting for transfers between devices, body(): weighted, cluster_mass = lax.psum((partial_sums, partial_mass), 'dp')  36.8 us
    gather x1, local copies, waits for them, and re-layouts, body(): send_codes = jnp.where(own_filled[:, None], code_items[own_safe], 0.0)  28 us
    all_gather x1, blocking collectives, body(): lax.all_gather(parents, 'clus', axis=0, tiled=True)  26.7 us
  transfers between devices with their start and end apart: 5, of which 4 were waited for; matrix products, arithmetic and copies ran while one was open for 25% of the time, Pallas kernels for 0%

commit v1 on v0

v1 whole, which is shorter than its diff:
```python
import jax
import jax.numpy as jnp
from jax import lax
from jax.experimental import pallas as pl
from jax.experimental.pallas import tpu as pltpu
from jax.sharding import PartitionSpec as P

F32, BF16, I32 = jnp.float32, jnp.bfloat16, jnp.int32
VMEM_LIMIT = 60 << 20


def strict_upper(size):
    row = lax.broadcasted_iota(I32, (size, size), 0)
    column = lax.broadcasted_iota(I32, (size, size), 1)
    return jnp.where(row < column, 1.0, 0.0).astype(BF16)


def score_kernel(first_ref, temper_ref, meta_ref, rows_ref, w_ref,
                 g_ref, e_ref, pay_ref, stat_ref, child_ref, upper_ref):
    group, parents, rows = meta_ref.shape
    blocks, depth, width = w_ref.shape
    size = width // 3
    slots = stat_ref.shape[1]
    first = first_ref[0]

    @pl.when(pl.program_id(0) == 0)
    def _():
        upper_ref[...] = strict_upper(rows)

    slot_id = lax.broadcasted_iota(I32, (slots, rows), 0).astype(F32)
    lane = lax.broadcasted_iota(I32, (slots, 128), 1)

    @pl.loop(0, group)
    def _(s):
        packed = meta_ref[s]
        block = lax.shift_right_logical(packed, 1) - first
        child = (packed & 1).astype(F32)
        hits, childs = [], []
        for b in range(blocks):
            match = block == b
            hits.append(jnp.sum(jnp.where(match, 1.0, 0.0), axis=0, keepdims=True))
            childs.append(jnp.sum(jnp.where(match, child, 0.0), axis=0, keepdims=True))
        hit = jnp.concatenate(hits, axis=0)
        rank = jnp.dot(hit.astype(BF16), upper_ref[...], preferred_element_type=F32)
        rank = jnp.where(hit > 0.0, rank, -1.0)
        selects = []
        child_lanes = jnp.zeros((slots, 128), F32)
        for b in range(blocks):
            select = slot_id == rank[b:b + 1]
            column = jnp.sum(jnp.where(select, childs[b], 0.0), axis=1, keepdims=True)
            child_lanes = jnp.where(lane == b, column, child_lanes)
            selects.append(jnp.where(select, 1.0, 0.0).astype(BF16))
        select = jnp.concatenate(selects, axis=0)
        source_rows = rows_ref[pl.ds(pl.multiple_of(s * rows, rows), rows), :]
        gathered = jnp.dot(select, source_rows, preferred_element_type=F32).astype(BF16)
        place = pl.ds(pl.multiple_of(s * slots, slots), slots)
        child_ref[place, :] = child_lanes
        for b in range(blocks):
            g_ref[b, place, :] = gathered[b * slots:(b + 1) * slots]

    wide_lane = lax.broadcasted_iota(I32, (group * slots, 128), 1)
    stats = jnp.zeros((group * slots, 128), F32)
    for b in range(blocks):
        product = jnp.dot(g_ref[b], w_ref[b], preferred_element_type=F32)
        score = product[:, :size] * temper_ref[b]
        deeper = jnp.where(
            child_ref[:, b:b + 1] > 0.5, product[:, 2 * size:], product[:, size:2 * size]
        ).astype(BF16)
        most = jnp.max(score, axis=1, keepdims=True)
        weight = jnp.exp(score - most)
        stats = jnp.where(wide_lane == b, most, stats)
        stats = jnp.where(wide_lane == 64 + b, jnp.sum(weight, axis=1, keepdims=True), stats)
        e_ref[b] = weight
        weight = weight.astype(BF16)
        for s in range(group):
            pay_ref[s, b * slots:(b + 1) * slots, :size] = weight[s * slots:(s + 1) * slots]
            pay_ref[s, b * slots:(b + 1) * slots, size:] = deeper[s * slots:(s + 1) * slots]
    for s in range(group):
        stat_ref[s] = stats[s * slots:(s + 1) * slots]


def combine_kernel(packed_ref, most_ref, sum_ref, back_ref, scale_ref, mass_ref, slot_ref,
                   rank_ref, dense_ref, part_ref):
    parents, rows = packed_ref.shape
    all_blocks, slots = most_ref.shape
    block = lax.shift_right_logical(packed_ref[...], 1)
    number = lax.broadcasted_iota(I32, (all_blocks, rows), 0)
    hit = jnp.zeros((all_blocks, rows), F32)
    for j in range(parents):
        hit = hit + jnp.where(block[j:j + 1] == number, 1.0, 0.0)
    rank = jnp.dot(hit.astype(BF16), strict_upper(rows), preferred_element_type=F32)
    rank_ref[...] = jnp.where(hit > 0.0, rank, -1.0)

    @pl.loop(0, all_blocks // 8)
    def _(i):
        here = pl.ds(pl.multiple_of(i * 8, 8), 8)
        rank = rank_ref[here, :]
        most, total = most_ref[here, :], sum_ref[here, :]
        dense_most = jnp.full((8, rows), -3e38, F32)
        dense_sum = jnp.zeros((8, rows), F32)
        for k in range(slots):
            match = rank == k
            dense_most = jnp.where(match, most[:, k:k + 1], dense_most)
            dense_sum = jnp.where(match, total[:, k:k + 1], dense_sum)
        dense_ref[here, :] = dense_most
        part_ref[here, :] = dense_sum

    rank = rank_ref[...]
    top = jnp.max(dense_ref[...], axis=0, keepdims=True)
    weight = jnp.where(rank >= 0.0, jnp.exp(dense_ref[...] - top), 0.0)
    total = jnp.sum(weight * part_ref[...], axis=0, keepdims=True)
    scale = weight / total
    dense_ref[...] = scale
    part_ref[...] = scale * part_ref[...]
    for j in range(parents):
        match = block[j:j + 1] == number
        scale_ref[j:j + 1, :] = jnp.sum(jnp.where(match, dense_ref[...], 0.0), axis=0, keepdims=True)
        mass_ref[j:j + 1, :] = jnp.sum(jnp.where(match, part_ref[...], 0.0), axis=0, keepdims=True)
        place = jnp.where(match, number.astype(F32) * slots + rank_ref[...], 0.0)
        slot_ref[j:j + 1, :] = jnp.sum(place, axis=0, keepdims=True).astype(I32)
    lane = lax.broadcasted_iota(I32, (8, slots), 1)

    @pl.loop(0, all_blocks // 8)
    def _(i):
        here = pl.ds(pl.multiple_of(i * 8, 8), 8)
        rank, scale = rank_ref[here, :], dense_ref[here, :]
        back = jnp.zeros((8, slots), F32)
        for k in range(slots):
            column = jnp.sum(jnp.where(rank == k, scale, 0.0), axis=1, keepdims=True)
            back = jnp.where(lane == k, column, back)
        back_ref[here, :] = back


def sum_kernel(scale_ref, e_ref, g_ref, weighted_ref, mass_ref):
    b = pl.program_id(0)
    lane = lax.broadcasted_iota(I32, scale_ref.shape, 1)
    scale = jnp.sum(jnp.where(lane == b, scale_ref[...], 0.0), axis=1, keepdims=True)
    codes = e_ref[0] * scale
    mass_ref[0] = jnp.sum(codes, axis=0, keepdims=True)
    weighted_ref[0] = lax.dot_general(
        codes.astype(BF16), g_ref[0], (((0,), (0,)), ((), ())), preferred_element_type=F32
    )


def spread_kernel(slot_ref, scale_ref, mass_ref, pay_ref, codes_ref, deeper_ref, wide_ref, code_ref, deep_ref):
    rows, parents = scale_ref.shape
    size = pay_ref.shape[1] // 2
    count = pay_ref.shape[0]
    chunk = min(512, count)

    @pl.loop(0, count // chunk)
    def _(i):
        here = pl.ds(pl.multiple_of(i * chunk, chunk), chunk)
        wide_ref[here, :] = pay_ref[here, :].astype(F32)

    @pl.loop(0, rows // 16)
    def _(i):
        for r in range(16):
            for j in range(parents):
                slot = slot_ref[(i * 16 + r) * parents + j]
                item = wide_ref[pl.ds(slot, 1), :]
                code_ref[r:r + 1, j * size:(j + 1) * size] = item[:, :size]
                deep_ref[r:r + 1, j * size:(j + 1) * size] = item[:, size:]
        here = pl.ds(pl.multiple_of(i * 16, 16), 16)
        scale, mass = scale_ref[here, :], mass_ref[here, :]
        for j in range(parents):
            part = slice(j * size, (j + 1) * size)
            codes_ref[here, part] = (code_ref[:, part] * scale[:, j:j + 1]).astype(BF16)
            deeper_ref[here, part] = deep_ref[:, part] * (parents * mass[:, j:j + 1])


def params():
    return pltpu.CompilerParams(vmem_limit_bytes=VMEM_LIMIT)


def whole(shape):
    return pl.BlockSpec(shape, lambda *_: (0,) * len(shape))


def body(embeddings, parents, children, temper, level_two, level_three):
    rows, depth = embeddings.shape
    count = parents.shape[1]
    blocks = temper.shape[0]
    size = level_two.shape[0] // blocks
    kinds = level_three.shape[0] // (blocks * size)
    assert kinds == 2
    shards = lax.axis_size("clus")
    own = lax.axis_index("clus")
    all_blocks = blocks * shards
    slots = 2 * rows * count // all_blocks
    group = min(8, shards)

    packed = (parents * kinds + children).T
    all_rows = lax.all_gather(embeddings, "clus", axis=0, tiled=True)
    all_packed = lax.all_gather(packed, "clus", axis=0, tiled=False)
    table = jnp.concatenate(
        [level_two.reshape(blocks, size, depth), level_three.reshape(blocks, kinds * size, depth)], axis=1
    ).transpose(0, 2, 1)
    first = (own * blocks).reshape(1).astype(I32)

    gathered, weights, pay, stats = pl.pallas_call(
        score_kernel,
        grid=(shards // group,),
        in_specs=[
            pl.BlockSpec(memory_space=pltpu.SMEM),
            pl.BlockSpec(memory_space=pltpu.SMEM),
            pl.BlockSpec((group, count, rows), lambda i: (i, 0, 0)),
            pl.BlockSpec((group * rows, depth), lambda i: (i, 0)),
            pl.BlockSpec(table.shape, lambda i: (0, 0, 0), pipeline_mode=pl.Buffered(1)),
        ],
        out_specs=[
            pl.BlockSpec((blocks, group * slots, depth), lambda i: (0, i, 0)),
            pl.BlockSpec((blocks, group * slots, size), lambda i: (0, i, 0)),
            pl.BlockSpec((group, blocks * slots, 2 * size), lambda i: (i, 0, 0)),
            pl.BlockSpec((group, slots, 128), lambda i: (i, 0, 0)),
        ],
        out_shape=[
            jax.ShapeDtypeStruct((blocks, shards * slots, depth), BF16),
            jax.ShapeDtypeStruct((blocks, shards * slots, size), F32),
            jax.ShapeDtypeStruct((shards, blocks * slots, 2 * size), BF16),
            jax.ShapeDtypeStruct((shards, slots, 128), F32),
        ],
        scratch_shapes=[pltpu.VMEM((group * slots, 128), F32), pltpu.VMEM((rows, rows), BF16)],
        compiler_params=params(),
    )(first, temper, all_packed, all_rows, table)

    returned = lax.all_to_all(pay, "clus", split_axis=0, concat_axis=0, tiled=True)
    kept = jnp.concatenate([stats[:, :, :blocks], stats[:, :, 64:64 + blocks]], axis=2)
    kept = lax.all_to_all(kept, "clus", split_axis=0, concat_axis=0, tiled=True)
    kept = kept.transpose(0, 2, 1)
    most = kept[:, :blocks].reshape(all_blocks, slots)
    sums = kept[:, blocks:].reshape(all_blocks, slots)

    back, scale, mass, place = pl.pallas_call(
        combine_kernel,
        out_shape=[
            jax.ShapeDtypeStruct((all_blocks, slots), F32),
            jax.ShapeDtypeStruct((count, rows), F32),
            jax.ShapeDtypeStruct((count, rows), F32),
            jax.ShapeDtypeStruct((count, rows), I32),
        ],
        scratch_shapes=[pltpu.VMEM((all_blocks, rows), F32)] * 3,
        compiler_params=params(),
    )(packed, most, sums)

    scales = lax.all_to_all(
        back.reshape(shards, blocks, slots), "clus", split_axis=0, concat_axis=0, tiled=True
    )
    scales = scales.transpose(0, 2, 1).reshape(shards * slots, blocks)

    partial, partial_mass = pl.pallas_call(
        sum_kernel,
        grid=(blocks,),
        in_specs=[
            whole(scales.shape),
            pl.BlockSpec((1, shards * slots, size), lambda i: (i, 0, 0)),
            pl.BlockSpec((1, shards * slots, depth), lambda i: (i, 0, 0)),
        ],
        out_specs=[
            pl.BlockSpec((1, size, depth), lambda i: (i, 0, 0)),
            pl.BlockSpec((1, 1, size), lambda i: (i, 0, 0)),
        ],
        out_shape=[
            jax.ShapeDtypeStruct((blocks, size, depth), F32),
            jax.ShapeDtypeStruct((blocks, 1, size), F32),
        ],
        compiler_params=params(),
    )(scales, weights, gathered)

    soft_codes, candidate_scores = pl.pallas_call(
        spread_kernel,
        in_specs=[
            pl.BlockSpec(memory_space=pltpu.SMEM),
            whole((rows, count)),
            whole((rows, count)),
            whole((all_blocks * slots, 2 * size)),
        ],
        out_shape=[
            jax.ShapeDtypeStruct((rows, count * size), BF16),
            jax.ShapeDtypeStruct((rows, count * size), F32),
        ],
        scratch_shapes=[
            pltpu.VMEM((all_blocks * slots, 2 * size), F32),
            pltpu.VMEM((16, count * size), F32),
            pltpu.VMEM((16, count * size), F32),
        ],
        compiler_params=params(),
    )(place.T.reshape(-1), scale.T, mass.T, returned.reshape(all_blocks * slots, 2 * size))

    weighted, cluster_mass = lax.psum((partial, partial_mass), "dp")
    cluster_mass = cluster_mass.reshape(blocks * size)
    new_centroids = weighted.reshape(blocks * size, depth) / jnp.maximum(cluster_mass, 1.0)[:, None]
    return soft_codes, candidate_scores, new_centroids, cluster_mass


def solution(mesh):
    rows = P(("dp", "clus"), None)
    return jax.shard_map(
        body,
        mesh=mesh,
        in_specs=(rows, rows, rows, P("clus"), P("clus", None), P("clus", None)),
        out_specs=(rows, rows, P("clus", None), P("clus")),
        check_vma=False,
    )
```

time: 820 us -> 327 us (0.40); the launches traced: 807 us -> 326 us
  local copies, waits for them, and re-layouts: 430 us -> 17.3 us
  matrix products: 98.9 us -> 0 us
  Pallas kernels: 0 us -> 79.8 us
  starting transfers between devices: 72 us -> 6.12 us
  waiting for transfers between devices: 104 us -> 134 us
  other arithmetic: 28.1 us -> 12.1 us
    gather x6 -> x0, local copies, waits for them, and re-layouts: 375 us -> none  [the longest x1 272 us: body(): jnp.take(all_rows, safe_item // parent_count, axis=0)]
    dot_general x10 -> x0, matrix products: 98.9 us -> none  [the longest x2 39.6 us: body(): jnp.einsum('sbmd,bcd->sbmc', slot_rows, third[:, child], preferred_elemen...]
    pallas_call x0 -> x4, Pallas kernels: none -> 79.8 us  [the longest x1 38.3 us: body(): pl.pallas_call(score_kernel, grid=(shards // group,), in_specs=[pl.BlockS...]
    all_gather x1, waiting for transfers between devices: 0.02 us -> 75.3 us  [body(): all_rows = lax.all_gather(embeddings, 'clus', axis=0, tiled=True)]
    all_to_all x3 -> x1, starting transfers between devices: 71.9 us -> 6.04 us  [body(): lax.all_to_all(pay, 'clus', split_axis=0, concat_axis=0, tiled=True)]
    all_to_all x3 -> x1, waiting for transfers between devices: 66.1 us -> 36.3 us  [body(): lax.all_to_all(pay, 'clus', split_axis=0, concat_axis=0, tiled=True)]
    all_to_all x0 -> x2, blocking collectives: none -> 22.4 us  [the longest x1 11.6 us: body(): kept = lax.all_to_all(kept, 'clus', split_axis=0, concat_axis=0, tiled=True)]
    all_gather x2 -> x1, blocking collectives: 50.7 us -> 29.1 us  [body(): all_packed = lax.all_gather(packed, 'clus', axis=0, tiled=False)]
  transfers between devices with their start and end apart: 5 -> 3, of which waited for: 4 -> 3; matrix products, arithmetic and copies ran while one was open for 25% -> 5% of each run, Pallas kernels for 0% -> 4%
where the time goes in v1:
time: 327 us; the launch traced here: 326 us
  waiting for transfers between devices  134 us (41%)
  Pallas kernels  79.8 us (24%)
  blocking collectives  62.4 us (19%)
  local copies, waits for them, and re-layouts  17.3 us (5%)
  between operations  14.2 us (4%)
  other arithmetic  12.1 us (4%)
  starting transfers between devices  6.12 us (2%)
    all_gather x1, waiting for transfers between devices, body(): all_rows = lax.all_gather(embeddings, 'clus', axis=0, tiled=True)  75.3 us
    pallas_call x1, Pallas kernels, body(): pl.pallas_call(score_kernel, grid=(shards // group,), in_specs=[pl.BlockS...  38.3 us
    all_to_all x1, waiting for transfers between devices, body(): lax.all_to_all(pay, 'clus', split_axis=0, concat_axis=0, tiled=True)  36.3 us
    all_gather x1, blocking collectives, body(): all_packed = lax.all_gather(packed, 'clus', axis=0, tiled=False)  29.1 us
    psum x1, waiting for transfers between devices, body(): weighted, cluster_mass = lax.psum((partial, partial_mass), 'dp')  21.4 us
    pallas_call x1, Pallas kernels, body(): pl.pallas_call(spread_kernel, in_specs=[pl.BlockSpec(memory_space=pltpu.S...  14.2 us
    pallas_call x1, Pallas kernels, body(): pl.pallas_call(combine_kernel, out_shape=[jax.ShapeDtypeStruct((all_block...  14.1 us
    pallas_call x1, Pallas kernels, body(): pl.pallas_call(sum_kernel, grid=(blocks,), in_specs=[whole(scales.shape),...  13.2 us
  transfers between devices with their start and end apart: 3, of which 3 were waited for; matrix products, arithmetic and copies ran while one was open for 5% of the time, Pallas kernels for 4%

profile of v1, /device:TPU:8, one launch (start us, length us, event | category | flops | bytes accessed | tf_op | source)
XLA Modules:
  0.0 325.6 jit_solution(2606935378100893209)
XLA Ops:
  7.2 0.7 all-gather.3.cloned.1.call-update
  7.9 6.4 %copy.24 = bf16[8,256,1024]{1,2,0:T(8,128)(2,1)} copy(bf16[8,256,1024]{2,1,0:T(8,128)(2,1)} %bitcast.26) | data formatting | bytes 8388608 | tf_op jit(solution)/shard_map/reshape | solution.py:197
  14.4 3.1 copy.23
  17.5 29.1 %all-gather = s32[256,512]{1,0:T(8,128)} all-gather(s32[8,512]{1,0:T(8,128)S(1)} %add_bitcast_fusion.packed_ref), channel_id=2, replica_groups=mesh['dp'=4,'clus'=32] {'clus'}, dimensions={0}, use_global_device_ids=true | all-gather | bytes 540672 | tf_op jit(solution)/shard_map/all_gather | solution.py:195
  46.6 5.6 %maximum_bitcast_fusion.w_ref = bf16[8,1024,384]{2,1,0:T(8,128)(2,1)} fusion(bf16[8,256,1024]{1,2,0:T(8,128)(2,1)} %copy.24, bf16[8,128,1024]{1,2,0:T(8,128)(2,1)S(1)} %copy.23), kind=kLoop, calls=%fused_computation | loop fusion | flops 12582912 | bytes 12582912 | tf_op jit(solution)/shard_map/transpose | solution.py:198
  52.3 75.3 %all-gather.3.cloned.1.call-done.rows_ref = bf16[16384,1024]{1,0:T(8,128)(2,1)} async-done(((bf16[512,1024]{1,0:T(8,128)(2,1)}), bf16[16384,1024]{1,0:T(8,128)(2,1)}) %all-gather.3.cloned.1.call-update) | async-done | bytes 33554448 | tf_op jit(solution)/shard_map/all_gather | solution.py:194
  127.6 38.3 %shard_map.93 = (bf16[8,1024,1024]{2,1,0:T(8,128)(2,1)}, f32[8,1024,128]{2,1,0:T(8,128)}, bf16[32,256,256]{2,1,0:T(8,128)(2,1)}, f32[32,32,128]{2,1,0:T(8,128)}) custom-call(s32[1]{0:T(128)} %bitcast.1.first_ref, f32[8]{0:T(128)} %temper_ref.1, s32[32,8,512]{2,1,0:T(8,128)} %bitcast.28, bf16[16384,1024]{1,0:T(8,128)(2,1)} %all-gather.3.cloned.1.call-done.rows_ref, ...), custom_call_target="tpu_custom_call" | custom-call | tf_op jit(solution)/shard_map/pallas_call | solution.py:201
  165.9 1.4 fusion
  167.3 0.2 pad_maximum_fusion
  167.6 0.2 copy.25
  167.8 0.2 reshape.58
  167.9 11.6 %all_to_all.15 = f32[32,1,512]{2,1,0:T(1,128)S(1)} all-to-all(f32[32,1,512]{2,1,0:T(1,128)S(1)} %reshape.58), channel_id=1, replica_groups=mesh['dp'=4,'clus'=32] {'clus'}, dimensions={0} | all-to-all | bytes 131072 | tf_op jit(solution)/shard_map/all_to_all | solution.py:229
  179.6 0.5 broadcast.4
  180.1 0.8 reduce
  180.9 0.1 reshape.59
  181.0 0.7 slice_bitcast_fusion
  181.8 14.1 %shard_map.94 = (f32[256,32]{1,0:T(8,128)}, f32[8,512]{1,0:T(8,128)}, f32[8,512]{1,0:T(8,128)}, s32[8,512]{1,0:T(8,128)}) custom-call(s32[8,512]{1,0:T(8,128)} %copy-done, f32[256,32]{1,0:T(8,128)} %get-tuple-element.31.most_ref, f32[256,32]{1,0:T(8,128)} %get-tuple-element.30.sum_ref), custom_call_target="tpu_custom_call" | custom-call | tf_op jit(solution)/shard_map/pallas_call | solution.py:234
  195.8 1.0 reshape.60
  196.9 10.8 %all_to_all.16 = f32[32,1,256]{2,1,0:T(1,128)S(1)} all-to-all(f32[32,1,256]{2,1,0:T(1,128)S(1)} %reshape.60), channel_id=1, replica_groups=mesh['dp'=4,'clus'=32] {'clus'}, dimensions={0} | all-to-all | bytes 65536 | tf_op jit(solution)/shard_map/all_to_all | solution.py:246
  207.7 0.7 reduce.1
  208.5 1.0 copy.29
  209.5 13.2 %shard_map.96 = (f32[8,128,1024]{2,1,0:T(8,128)}, f32[8,1,128]{2,1,0:T(1,128)}) custom-call(f32[1024,8]{1,0:T(8,128)} %bitcast.30, f32[8,1024,128]{2,1,0:T(8,128)} %get-tuple-element.24.e_ref, bf16[8,1024,1024]{2,1,0:T(8,128)(2,1)} %get-tuple-element.25.g_ref), custom_call_target="tpu_custom_call" | custom-call | tf_op jit(solution)/shard_map/pallas_call | solution.py:251
  222.8 6.0 %all-to-all-start.1 = ((bf16[32,256,256]{2,1,0:T(8,128)(2,1)}), bf16[32,256,256]{2,1,0:T(8,128)(2,1)}, u32[]{:S(2)}, u32[]{:S(2)}) async-start(bf16[32,256,256]{2,1,0:T(8,128)(2,1)} %get-tuple-element.20), calls=%async_computation.1 | async-start | bytes 8388608 | tf_op jit(solution)/shard_map/all_to_all | solution.py:227
  228.8 0.1 copy.26
  228.9 0.7 reshape.51.slot_ref
  229.7 0.8 copy.27
  230.5 0.8 copy.28
  231.4 10.8 %psum.15 = f32[1024]{0:T(1024)S(1)} all-reduce(f32[1024]{0:T(1024)S(1)} %bitcast.37), channel_id=1, replica_groups=mesh['dp'=4,'clus'=32] {'dp'}, use_global_device_ids=true, to_apply=%region_1.0 | all-reduce | flops 1024 | bytes 8192 | tf_op jit(solution)/shard_map/psum | solution.py:290
  242.2 36.3 %all-to-all-done.1 = bf16[32,256,256]{2,1,0:T(8,128)(2,1)} async-done(((bf16[32,256,256]{2,1,0:T(8,128)(2,1)}), bf16[32,256,256]{2,1,0:T(8,128)(2,1)}, u32[]{:S(2)}, u32[]{:S(2)}) %all-to-all-start.1) | async-done | bytes 4194336 | tf_op jit(solution)/shard_map/all_to_all | solution.py:227
  278.5 14.2 %shard_map.95 = (bf16[512,1024]{1,0:T(8,128)(2,1)}, f32[512,1024]{1,0:T(8,128)}) custom-call(s32[4096]{0:T(1024)} %reshape.51.slot_ref, f32[512,8]{1,0:T(8,128)} %bitcast.32, f32[512,8]{1,0:T(8,128)} %bitcast.33, bf16[8192,256]{1,0:T(8,128)(2,1)} %bitcast.12.pay_ref), custom_call_target="tpu_custom_call" | custom-call | tf_op jit(solution)/shard_map/pallas_call | solution.py:270
  292.7 21.4 %all-reduce.2.cloned.1.call-done = f32[1024,1024]{1,0:T(8,128)} async-done(((f32[1024,1024]{1,0:T(8,128)}), f32[1024,1024]{1,0:T(8,128)}) %all-reduce.2.cloned.1.call-update) | async-done | bytes 4194320 | tf_op jit(solution)/shard_map/psum | solution.py:290
  314.1 4.7 %broadcast_divide_fusion = f32[1024,1024]{1,0:T(8,128)} fusion(f32[1024,1024]{1,0:T(8,128)} %all-reduce.2.cloned.1.call-done, f32[1024]{0:T(1024)S(1)} %broadcast_maximum_fusion), kind=kLoop, calls=%fused_computation.1 | loop fusion | flops 1048576 | bytes 8392704 | tf_op jit(solution)/shard_map/div | solution.py:292
  (23 shorter events, 0.2 us)
Async XLA Ops:
  7.2 120.4 %all-gather.3.cloned.1.call-start = ((), (), s32[]{:S(2)}) async-start(), calls=%async_computation.3 | async-start | bytes 34603008 | tf_op jit(solution)/shard_map/all_gather | solution.py:194
  7.9 306.2 %all-reduce.2.cloned.1.call-start = ((), (), s32[]{:S(2)}) async-start(), calls=%async_computation.4 | async-start | bytes 8388608 | tf_op jit(solution)/shard_map/psum | solution.py:290
  14.4 3.1 copy-start.1
  14.4 3.1 copy-start.2
  17.5 34.8 %copy-start = (s32[8,512]{1,0:T(8,128)}, s32[8,512]{1,0:T(8,128)S(1)}, u32[]{:S(2)}) copy-start(s32[8,512]{1,0:T(8,128)S(1)} %add_bitcast_fusion.packed_ref) | copy-start | bytes 49156
  222.7 6.1 %copy-start.5 = (s32[8,512]{1,0:T(8,128)S(1)}, s32[8,512]{1,0:T(8,128)}, u32[]{:S(2)}) copy-start(s32[8,512]{1,0:T(8,128)} %get-tuple-element.17) | copy-start | bytes 49156
  222.7 7.0 %copy-start.4 = (f32[8,512]{1,0:T(8,128)S(1)}, f32[8,512]{1,0:T(8,128)}, u32[]{:S(2)}) copy-start(f32[8,512]{1,0:T(8,128)} %get-tuple-element.18) | copy-start | bytes 49156
  222.7 7.8 %copy-start.3 = (f32[8,512]{1,0:T(8,128)S(1)}, f32[8,512]{1,0:T(8,128)}, u32[]{:S(2)}) copy-start(f32[8,512]{1,0:T(8,128)} %get-tuple-element.19) | copy-start | bytes 49156
  222.7 8.6 %copy-start.7 = (f32[8,1,128]{2,1,0:T(1,128)S(1)}, f32[8,1,128]{2,1,0:T(1,128)}, u32[]{:S(2)}) copy-start(f32[8,1,128]{2,1,0:T(1,128)} %get-tuple-element.27) | copy-start | bytes 12292
  222.8 55.7 %all-to-all-start.1 = ((bf16[32,256,256]{2,1,0:T(8,128)(2,1)}), bf16[32,256,256]{2,1,0:T(8,128)(2,1)}, u32[]{:S(2)}, u32[]{:S(2)}) async-start(bf16[32,256,256]{2,1,0:T(8,128)(2,1)} %get-tuple-element.20), calls=%async_computation.1 | async-start | bytes 8388608 | tf_op jit(solution)/shard_map/all_to_all | solution.py:227
  242.2 76.6 %copy-start.6 = (f32[1024]{0:T(1024)}, f32[1024]{0:T(1024)S(1)}, u32[]{:S(2)}) copy-start(f32[1024]{0:T(1024)S(1)} %psum.15) | copy-start | bytes 12292
Sparse Core Ops, SparseCore 0:
  10.2 117.3 all-gather.2
  222.8 91.1 all-reduce.1

commit v2 on v1

v2 whole, which is shorter than its diff:
```python
import jax
import jax.numpy as jnp
from jax import lax
from jax.experimental import pallas as pl
from jax.experimental.pallas import tpu as pltpu
from jax.sharding import PartitionSpec as P

F32, BF16, I32 = jnp.float32, jnp.bfloat16, jnp.int32
MESH = pl.DeviceIdType.MESH
VMEM_LIMIT = 60 << 20

ORDER = (
    (0, 0), (1, 0), (3, 0), (0, 1), (0, 3), (2, 0), (0, 2), (1, 1),
    (3, 3), (3, 1), (1, 3), (2, 1), (2, 3), (1, 2), (3, 2), (2, 2),
)
WAVES = (0, 12, 24, 32)
RING = (0, 1, 3, 2)


def packed_table(values):
    word = sum(v << (2 * i) for i, v in enumerate(values))
    return word - (1 << 32) if word >= 1 << 31 else word


TABLE_Y = packed_table([o[0] for o in ORDER])
TABLE_Z = packed_table([o[1] for o in ORDER])


def entry(table, index):
    return lax.shift_right_logical(jnp.int32(table), jnp.int32(2) * index) % 4


def strict_upper(size):
    row = lax.broadcasted_iota(I32, (size, size), 0)
    column = lax.broadcasted_iota(I32, (size, size), 1)
    return jnp.where(row < column, 1.0, 0.0).astype(BF16)


def three(x):
    high = x.astype(BF16)
    rest = x - high.astype(F32)
    middle = rest.astype(BF16)
    low = (rest - middle.astype(F32)).astype(BF16)
    return high, middle, low


def fused_kernel(
    temper_ref, ext_ref, packed_ref, two_ref, three_ref,
    buf_ref, ret_ref, scale_ref, mass_ref, slot_ref, fin_ref, total_ref,
    rowbuf, w2, w3, g, et, pay, child, upper, stats, stat_out, stat_in, onehot, item_rank, back_out, back_in,
    sc, part, relay_in, near_in, own, mass_all, mass_send, column_scr,
    load_sem, w_sem, local_sem, ring_send, ring_recv, sib_send, sib_recv, pay_send, pay_recv,
    stat_send, stat_recv, back_send, back_recv, dp_send, dp_recv,
):
    parents, rows = packed_ref.shape
    total_rows, depth = ext_ref.shape
    slots = 32
    blocks = temper_ref.shape[0]
    size = w2.shape[0] // blocks
    shards = buf_ref.shape[0]
    all_blocks = blocks * shards
    dp = lax.axis_index("dp")
    me = lax.axis_index("clus")
    core = me % 2
    z = (me // 2) % 4
    y = me // 8
    sibling = me + 1 - 2 * core

    def at(dy, dz, flip=0):
        return (((y + dy) % 4) * 4 + (z + dz) % 4) * 2 + (core + flip) % 2

    def source(p):
        q = p // 2
        return at(entry(TABLE_Y, q), entry(TABLE_Z, q), p % 2)

    def holder(p):
        q = p // 2
        return at(4 - entry(TABLE_Y, q), 4 - entry(TABLE_Z, q), p % 2)

    barrier = pltpu.get_barrier_semaphore()

    @pl.loop(1, shards)
    def _(d):
        pl.semaphore_signal(barrier, inc=1, device_id=(dp, (me + d) % shards), device_id_type=MESH)

    for d in (1, 2, 3):
        pl.semaphore_signal(barrier, inc=1, device_id=((dp + d) % 4, me), device_id_type=MESH)
    pl.semaphore_wait(barrier, shards - 1 + 3)

    quarter = rows // 4
    ids = total_rows - rows
    piece = {
        "A": (0, ids + 2 * quarter), "A0": (0, ids + quarter), "A1": (ids + quarter, quarter),
        "B": (ids + 2 * quarter, 2 * quarter), "B0": (ids + 2 * quarter, quarter), "B1": (ids + 3 * quarter, quarter),
    }

    def part_of(ref, name):
        start, length = piece[name]
        return ref.at[pl.ds(start, length), :]

    def chip(half, first, second):
        return (first, second) if half == "A" else (second, first)

    def ring(half, k, offset, name, step):
        index = (0 if half == "A" else 20) + k
        block = at(*offset)
        mine = ext_ref if offset == (0, 0) else buf_ref.at[block]
        return pltpu.make_async_remote_copy(
            src_ref=part_of(mine, name), dst_ref=part_of(buf_ref.at[block], name),
            send_sem=ring_send.at[index], recv_sem=ring_recv.at[index],
            device_id=(dp, at(*step)), device_id_type=MESH,
        )

    def arrival(half, k, offset, name):
        index = (0 if half == "A" else 20) + k
        block = at(*offset)
        return pltpu.make_async_remote_copy(
            src_ref=part_of(buf_ref.at[block], name), dst_ref=part_of(buf_ref.at[block], name),
            send_sem=ring_send.at[index], recv_sem=ring_recv.at[index],
            device_id=(dp, at(1, 0)), device_id_type=MESH,
        )

    sent = []

    def go(copy):
        copy.start()
        sent.append(copy)

    def share(half, offset):
        index = (0 if half == "A" else 16) + ORDER.index(offset)
        block = at(*offset)
        mine = ext_ref if offset == (0, 0) else buf_ref.at[block]
        go(pltpu.make_async_remote_copy(
            src_ref=part_of(mine, half), dst_ref=part_of(buf_ref.at[block], half),
            send_sem=sib_send.at[index], recv_sem=sib_recv.at[index],
            device_id=(dp, sibling), device_id_type=MESH,
        ))

    def shared(half, q):
        index = (0 if half == "A" else 16) + q
        block = at(*ORDER[q], 1)
        pltpu.make_async_remote_copy(
            src_ref=part_of(buf_ref.at[block], half), dst_ref=part_of(buf_ref.at[block], half),
            send_sem=sib_send.at[index], recv_sem=sib_recv.at[index],
            device_id=(dp, sibling), device_id_type=MESH,
        ).wait_recv()

    def first_axis(half, step):
        return chip(half, step, 0)

    def second_axis(half, step):
        return chip(half, 0, step)

    def enter_second(half, i):
        block = chip(half, RING[i], 0)
        go(ring(half, 4 + 4 * i, block, half, second_axis(half, 1)))
        go(ring(half, 5 + 4 * i, block, half, second_axis(half, 3)))

    def first_near(half):
        arrival(half, 1, chip(half, 1, 0), half).wait_recv()
        go(ring(half, 3, chip(half, 1, 0), half + "1", first_axis(half, 3)))
        arrival(half, 0, chip(half, 3, 0), half).wait_recv()
        go(ring(half, 2, chip(half, 3, 0), half + "0", first_axis(half, 1)))
        enter_second(half, 1)
        enter_second(half, 2)
        share(half, chip(half, 1, 0))
        share(half, chip(half, 3, 0))

    def first_far(half):
        arrival(half, 2, chip(half, 2, 0), half + "0").wait_recv()
        arrival(half, 3, chip(half, 2, 0), half + "1").wait_recv()
        enter_second(half, 3)
        share(half, chip(half, 2, 0))

    def second_near(half, i):
        o = RING[i]
        arrival(half, 5 + 4 * i, chip(half, o, 1), half).wait_recv()
        go(ring(half, 7 + 4 * i, chip(half, o, 1), half + "1", second_axis(half, 3)))
        arrival(half, 4 + 4 * i, chip(half, o, 3), half).wait_recv()
        go(ring(half, 6 + 4 * i, chip(half, o, 3), half + "0", second_axis(half, 1)))
        share(half, chip(half, o, 1))
        share(half, chip(half, o, 3))

    def second_far(half, i):
        o = RING[i]
        arrival(half, 6 + 4 * i, chip(half, o, 2), half + "0").wait_recv()
        arrival(half, 7 + 4 * i, chip(half, o, 2), half + "1").wait_recv()
        share(half, chip(half, o, 2))

    def load(p):
        return pltpu.make_async_copy(buf_ref.at[source(p)], rowbuf.at[p % 2], load_sem.at[p % 2])

    first_block = (me * blocks).astype(F32)

    def gather(low, high):
        for q in range(low // 2, high // 2):
            shared("A", q)
            shared("B", q)
        load(low).start()
        slot_id = lax.broadcasted_iota(I32, (slots, rows), 0).astype(F32)
        lane = lax.broadcasted_iota(I32, (slots, 128), 1)

        @pl.loop(low, high)
        def _(p):
            load(p).wait()

            @pl.when(p + 1 < high)
            def _():
                load(p + 1).start()

            meta = rowbuf[p % 2, 0:2 * parents, 0:rows].astype(F32)
            block = meta[:parents] - first_block
            kind = meta[parents:]
            hits, kinds = [], []
            for b in range(blocks):
                match = block == float(b)
                hits.append(jnp.sum(jnp.where(match, 1.0, 0.0), axis=0, keepdims=True))
                kinds.append(jnp.sum(jnp.where(match, kind, 0.0), axis=0, keepdims=True))
            hit = jnp.concatenate(hits, axis=0)
            rank = jnp.dot(hit.astype(BF16), upper[...], preferred_element_type=F32)
            rank = jnp.where(hit > 0.0, rank, -1.0)
            selects = []
            child_lanes = jnp.zeros((slots, 128), F32)
            for b in range(blocks):
                select = slot_id == rank[b:b + 1]
                column = jnp.sum(jnp.where(select, kinds[b], 0.0), axis=1, keepdims=True)
                child_lanes = jnp.where(lane == b, column, child_lanes)
                selects.append(jnp.where(select, 1.0, 0.0).astype(BF16))
            select = jnp.concatenate(selects, axis=0)
            picked = jnp.dot(
                select, rowbuf[p % 2, ids:total_rows, :], preferred_element_type=F32
            ).astype(BF16)
            place = pl.ds(pl.multiple_of(p * slots, slots), slots)
            child[place, :] = child_lanes
            for b in range(blocks):
                g[b, place, :] = picked[b * slots:(b + 1) * slots]

    contract_last = (((1,), (1,)), ((), ()))

    def score(wave, low, high):
        start, count = WAVES[wave] * slots, (WAVES[wave + 1] - WAVES[wave]) * slots
        here = slice(start, start + count)
        lane = lax.broadcasted_iota(I32, (count, 128), 1)

        @pl.loop(low, high)
        def _(b):
            x = g[b, here, :]
            near = lax.dot_general(
                x, w2[pl.ds(pl.multiple_of(b * size, size), size), :], contract_last, preferred_element_type=F32
            )
            far = lax.dot_general(
                x, w3[pl.ds(pl.multiple_of(b * 2 * size, 2 * size), 2 * size), :], contract_last,
                preferred_element_type=F32,
            )
            value = near * temper_ref[b]
            which = jnp.sum(jnp.where(lane == b, child[here, :], 0.0), axis=1, keepdims=True)
            deeper = jnp.where(which > 0.5, far[:, size:], far[:, :size]).astype(BF16)
            most = jnp.max(value, axis=1, keepdims=True)
            weight = jnp.exp(value - most)
            amount = jnp.sum(weight, axis=1, keepdims=True)
            old = stats[here, :]
            stats[here, :] = jnp.where(lane == b, most, jnp.where(lane == b + blocks, amount, old))
            et[b, :, here] = weight.T
            weight = weight.astype(BF16)
            place = pl.ds(pl.multiple_of(b * slots, slots), slots)
            for i in range(count // slots):
                pay[WAVES[wave] + i, place, 0:size] = weight[i * slots:(i + 1) * slots]
                pay[WAVES[wave] + i, place, size:2 * size] = deeper[i * slots:(i + 1) * slots]

    def each(low, high, action):
        @pl.loop(max(low, 1), high)
        def _(p):
            action(p)

    def stat_copy(p, index, device):
        return pltpu.make_async_remote_copy(
            src_ref=stat_out.at[p], dst_ref=stat_in.at[index], send_sem=stat_send.at[p], recv_sem=stat_recv.at[p],
            device_id=(dp, device), device_id_type=MESH,
        )

    def send_stats(wave):
        low, high = WAVES[wave], WAVES[wave + 1]
        for t in range(low // 4, high // 4):
            flipped = stats[t * 128:(t + 1) * 128, :].T[0:2 * blocks, :]
            for s in range(4):
                moved = flipped if s == 0 else pltpu.roll(flipped, 128 - s * slots, 1)
                stat_out[t * 4 + s] = moved
        if low == 0:
            stat_in[me] = stat_out[0]
        each(low, high, lambda p: stat_copy(p, me, source(p)).start())

    def pay_copy(p, index, device):
        return pltpu.make_async_remote_copy(
            src_ref=pay.at[p], dst_ref=ret_ref.at[index], send_sem=pay_send.at[p], recv_sem=pay_recv.at[p],
            device_id=(dp, device), device_id_type=MESH,
        )

    def send_pay(low, high):
        each(low, high, lambda p: pay_copy(p, me, source(p)).start())

    def back_copy(p, index, device):
        return pltpu.make_async_remote_copy(
            src_ref=back_out.at[index], dst_ref=back_in.at[p], send_sem=back_send.at[p], recv_sem=back_recv.at[p],
            device_id=(dp, device), device_id_type=MESH,
        )

    for half, step in (("A", 1), ("B", 1)):
        go(ring(half, 0, (0, 0), half, first_axis(half, 1)))
        go(ring(half, 1, (0, 0), half, first_axis(half, 3)))
    enter_second("A", 0)
    enter_second("B", 0)
    share("A", (0, 0))
    share("B", (0, 0))
    in_two = pltpu.make_async_copy(two_ref, w2, w_sem.at[0])
    in_three = pltpu.make_async_copy(three_ref, w3, w_sem.at[1])
    in_two.start()
    in_three.start()
    own_in = pltpu.make_async_copy(ext_ref, rowbuf.at[0], local_sem.at[0])
    own_in.start()
    upper[...] = strict_upper(rows)
    stats[...] = jnp.zeros_like(stats)
    back_out[...] = jnp.zeros_like(back_out)
    own_in.wait()
    own_out = pltpu.make_async_copy(rowbuf.at[0], buf_ref.at[me], local_sem.at[1])
    own_out.start()

    named = lax.shift_right_logical(packed_ref[...], 1)
    number = lax.broadcasted_iota(I32, (all_blocks, rows), 0)
    hit = jnp.zeros((all_blocks, rows), F32)
    for j in range(parents):
        one = jnp.where(named[j:j + 1] == number, 1.0, 0.0)
        hit = hit + one
        onehot[j] = one.astype(BF16)
    own_rank = jnp.dot(hit.astype(BF16), upper[...], preferred_element_type=F32)
    for j in range(parents):
        item_rank[j:j + 1, :] = jnp.sum(onehot[j].astype(F32) * own_rank, axis=0, keepdims=True)
    slot_ref[...] = named * slots + item_rank[...].astype(I32)
    own_out.wait()

    first_near("A")
    first_near("B")
    gather(0, 2)
    second_near("A", 0)
    second_near("B", 0)
    first_far("A")
    first_far("B")
    gather(2, 6)
    second_far("A", 0)
    second_far("B", 0)
    second_near("A", 1)
    second_near("B", 1)
    gather(6, 12)
    in_two.wait()
    in_three.wait()
    second_near("A", 2)
    second_near("B", 2)
    score(0, 0, blocks)
    second_far("A", 1)
    second_far("B", 1)
    send_stats(0)
    gather(12, 18)
    second_far("A", 2)
    second_far("B", 2)
    gather(18, 22)
    second_near("A", 3)
    second_near("B", 3)
    gather(22, 24)
    score(1, 0, blocks)
    send_stats(1)
    second_far("A", 3)
    second_far("B", 3)
    send_pay(0, PAY_CUTS[0])
    gather(24, 32)
    score(2, 0, blocks)
    send_stats(2)
    send_pay(PAY_CUTS[0], PAY_CUTS[1])
    own_pay = pltpu.make_async_copy(pay.at[0], ret_ref.at[me], local_sem.at[0])
    own_pay.start()

    each(0, shards, lambda p: stat_copy(p, holder(p), source(p)).wait_recv())
    table = jnp.concatenate([stat_in[o, 0:blocks, :] for o in range(shards)], axis=0)
    table_sum = jnp.concatenate([stat_in[o, blocks:2 * blocks, :] for o in range(shards)], axis=0)
    both = jnp.concatenate([table.T[0:slots], table_sum.T[0:slots]], axis=0)
    stack = jnp.concatenate(three(both), axis=0)
    slot_row = lax.broadcasted_iota(I32, (slots, rows), 0).astype(F32)
    mosts, amounts = [], []
    for j in range(parents):
        found = jnp.dot(stack, onehot[j], preferred_element_type=F32)
        found = (found[0:2 * slots] + found[2 * slots:4 * slots]) + found[4 * slots:6 * slots]
        pick = slot_row == item_rank[j:j + 1, :]
        mosts.append(jnp.sum(jnp.where(pick, found[0:slots], 0.0), axis=0, keepdims=True))
        amounts.append(jnp.sum(jnp.where(pick, found[slots:], 0.0), axis=0, keepdims=True))
    most = jnp.concatenate(mosts, axis=0)
    amount = jnp.concatenate(amounts, axis=0)
    weight = jnp.exp(most - jnp.max(most, axis=0, keepdims=True))
    scale = weight / jnp.sum(weight * amount, axis=0, keepdims=True)
    scale_ref[...] = scale
    mass_ref[...] = scale * amount
    back = jnp.zeros((all_blocks, 4 * slots), F32)
    for j in range(parents):
        pick = slot_row == item_rank[j:j + 1, :]
        spread = jnp.where(pick, scale[j:j + 1, :], 0.0)
        pad = jnp.zeros((slots, rows), BF16)
        stacked = jnp.concatenate(three(spread) + (pad,), axis=0)
        back = back + lax.dot_general(onehot[j], stacked, contract_last, preferred_element_type=F32)
    back = (back + pltpu.roll(back, 3 * slots, 1)) + pltpu.roll(back, 2 * slots, 1)
    for o in range(shards):
        back_out[o] = back[o * blocks:(o + 1) * blocks, :]
    back_in[0] = back_out[me]
    each(0, shards, lambda p: back_copy(p, holder(p), holder(p)).start())
    send_pay(PAY_CUTS[1], shards)
    each(0, shards, lambda p: back_copy(p, holder(p), holder(p)).wait_recv())
    lane8 = lax.broadcasted_iota(I32, (blocks, 128), 1)
    for t in range(shards // 4):
        joined = back_in[4 * t]
        for s in range(1, 4):
            joined = jnp.where(lane8 >= s * slots, pltpu.roll(back_in[4 * t + s], s * slots, 1), joined)
        sc[:, t * 128:(t + 1) * 128] = joined

    def sums(b):
        codes = et[b] * sc[pl.ds(b, 1), :]
        high = codes.astype(BF16)
        low = (codes - high.astype(F32)).astype(BF16)
        product = jnp.dot(jnp.concatenate([high, low], axis=0), g[b], preferred_element_type=F32)
        return product[:size] + product[size:], jnp.sum(codes, axis=1, keepdims=True)

    lane128 = lax.broadcasted_iota(I32, (size, 128), 1)
    column_scr[...] = jnp.zeros_like(column_scr)

    @pl.loop(0, blocks)
    def _(i):
        b = (2 * ((dp + 2) % 4) + i) % blocks
        value, column = sums(b)
        part[b] = value
        column_scr[...] = jnp.where(lane128 == b, column, column_scr[...])

    def dp_copy(index, source_ref, target_ref, step):
        return pltpu.make_async_remote_copy(
            src_ref=source_ref, dst_ref=target_ref, send_sem=dp_send.at[index], recv_sem=dp_recv.at[index],
            device_id=((dp + step) % 4, me), device_id_type=MESH,
        )

    right, left, across = (dp + 1) % 4, (dp + 3) % 4, (dp + 2) % 4
    mass_send[...] = column_scr[...].T[0:blocks, :]
    mass_all[dp] = mass_send[...]
    mass_copies = [dp_copy(8 + d, mass_send, mass_all.at[dp], d) for d in (1, 2, 3)]
    for copy in mass_copies:
        copy.start()
    half_part = near_in
    own[0] = part[2 * across].astype(BF16)
    own[1] = part[2 * across + 1].astype(BF16)
    relay = [dp_copy(0, own.at[0], relay_in.at[0], 1), dp_copy(1, own.at[1], relay_in.at[1], 3)]
    for copy in relay:
        copy.start()
    own[3] = part[2 * right + 1].astype(BF16)
    own[4] = part[2 * left].astype(BF16)
    near = [
        dp_copy(2, own.at[2], half_part.at[0], 1), dp_copy(3, own.at[3], half_part.at[1], 1),
        dp_copy(4, own.at[4], half_part.at[2], 3), dp_copy(5, own.at[5], half_part.at[3], 3),
    ]
    near[1].start()
    near[2].start()
    relay[0].wait_recv()
    own[2] = (part[2 * right] + relay_in[0].astype(F32)).astype(BF16)
    near[0].start()
    relay[1].wait_recv()
    own[5] = (part[2 * left + 1] + relay_in[1].astype(F32)).astype(BF16)
    near[3].start()
    for copy in mass_copies:
        copy.wait_recv()
    all_mass = ((mass_all[0] + mass_all[1]) + mass_all[2]) + mass_all[3]
    total_ref[...] = all_mass
    spare = jnp.zeros((128 - blocks, 128), F32)
    column_scr[...] = jnp.maximum(jnp.concatenate([all_mass, spare], axis=0), 1.0).T
    for copy in near:
        copy.wait_recv()
    for i in range(2):
        b = 2 * dp + i
        column = jnp.sum(jnp.where(lane128 == b, column_scr[...], 0.0), axis=1, keepdims=True)
        value = part[b] + (half_part[i].astype(F32) + half_part[2 + i].astype(F32))
        own[6 + i] = (value / column).astype(BF16)
    ready = [
        dp_copy(12, own.at[6], fin_ref.at[2 * dp], 1), dp_copy(13, own.at[7], fin_ref.at[2 * dp + 1], 3),
        dp_copy(14, own.at[7], fin_ref.at[2 * dp + 1], 1), dp_copy(15, own.at[6], fin_ref.at[2 * dp], 3),
    ]
    for copy in ready:
        copy.start()
    own_fin = [pltpu.make_async_copy(own.at[6 + i], fin_ref.at[2 * dp + i], local_sem.at[2 + i]) for i in range(2)]
    for copy in own_fin:
        copy.start()
    dp_copy(12, own.at[6], fin_ref.at[2 * left], 1).wait_recv()
    onward = [dp_copy(6, fin_ref.at[2 * left], fin_ref.at[2 * left], 1)]
    onward[0].start()
    dp_copy(13, own.at[7], fin_ref.at[2 * right + 1], 3).wait_recv()
    onward.append(dp_copy(7, fin_ref.at[2 * right + 1], fin_ref.at[2 * right + 1], 3))
    onward[1].start()
    dp_copy(14, own.at[7], fin_ref.at[2 * left + 1], 1).wait_recv()
    dp_copy(15, own.at[6], fin_ref.at[2 * right], 3).wait_recv()
    dp_copy(6, own.at[6], fin_ref.at[2 * across], 1).wait_recv()
    dp_copy(7, own.at[7], fin_ref.at[2 * across + 1], 3).wait_recv()

    each(0, shards, lambda p: pay_copy(p, holder(p), source(p)).wait_recv())
    for copy in sent + mass_copies + relay + near + ready + onward:
        copy.wait_send()
    each(0, shards, lambda p: pay_copy(p, me, source(p)).wait_send())
    each(0, shards, lambda p: stat_copy(p, me, source(p)).wait_send())
    each(0, shards, lambda p: back_copy(p, holder(p), holder(p)).wait_send())
    own_pay.wait()
    for copy in own_fin:
        copy.wait()


PAY_CUTS = (8, 16)


def spread_kernel(slot_ref, scale_ref, mass_ref, pay_ref, codes_ref, deeper_ref, wide_ref, code_ref, deep_ref):
    rows, parents = scale_ref.shape
    size = pay_ref.shape[1] // 2
    count = pay_ref.shape[0]
    chunk = min(512, count)

    @pl.loop(0, count // chunk)
    def _(i):
        here = pl.ds(pl.multiple_of(i * chunk, chunk), chunk)
        wide_ref[here, :] = pay_ref[here, :].astype(F32)

    @pl.loop(0, rows // 16)
    def _(i):
        for r in range(16):
            for j in range(parents):
                slot = slot_ref[(i * 16 + r) * parents + j]
                item = wide_ref[pl.ds(slot, 1), :]
                code_ref[r:r + 1, j * size:(j + 1) * size] = item[:, :size]
                deep_ref[r:r + 1, j * size:(j + 1) * size] = item[:, size:]
        here = pl.ds(pl.multiple_of(i * 16, 16), 16)
        scale, mass = scale_ref[here, :], mass_ref[here, :]
        for j in range(parents):
            part = slice(j * size, (j + 1) * size)
            codes_ref[here, part] = (code_ref[:, part] * scale[:, j:j + 1]).astype(BF16)
            deeper_ref[here, part] = deep_ref[:, part] * (parents * mass[:, j:j + 1])


def params():
    return pltpu.CompilerParams(vmem_limit_bytes=VMEM_LIMIT)


def whole(shape):
    return pl.BlockSpec(shape, lambda *_: (0,) * len(shape))


def body(embeddings, parents, children, temper, level_two, level_three):
    rows, depth = embeddings.shape
    count = parents.shape[1]
    blocks = temper.shape[0]
    size = level_two.shape[0] // blocks
    kinds = level_three.shape[0] // (blocks * size)
    shards = lax.axis_size("clus")
    all_blocks = blocks * shards
    slots = 2 * rows * count // all_blocks
    assert kinds == 2 and shards == 32 and slots == 32 and blocks == 8 and lax.axis_size("dp") == 4

    packed = (parents * kinds + children).T
    ids = jnp.concatenate([parents.T, children.T], axis=0).astype(BF16)
    ids = jnp.pad(ids, ((0, 0), (0, depth - rows)))
    extended = jnp.concatenate([ids, embeddings], axis=0)
    total_rows = extended.shape[0]
    anywhere = pl.BlockSpec(memory_space=pl.ANY)
    vmem = pl.BlockSpec(memory_space=pltpu.VMEM)
    dma = pltpu.SemaphoreType.DMA

    _, returned, scale, mass, place, sums, cluster_mass = pl.pallas_call(
        fused_kernel,
        in_specs=[pl.BlockSpec(memory_space=pltpu.SMEM), anywhere, vmem, anywhere, anywhere],
        out_specs=[anywhere, anywhere, vmem, vmem, vmem, anywhere, vmem],
        out_shape=[
            jax.ShapeDtypeStruct((shards, total_rows, depth), BF16),
            jax.ShapeDtypeStruct((shards, blocks * slots, 2 * size), BF16),
            jax.ShapeDtypeStruct((count, rows), F32),
            jax.ShapeDtypeStruct((count, rows), F32),
            jax.ShapeDtypeStruct((count, rows), I32),
            jax.ShapeDtypeStruct((blocks, size, depth), BF16),
            jax.ShapeDtypeStruct((blocks, size), F32),
        ],
        scratch_shapes=[
            pltpu.VMEM((2, total_rows, depth), BF16),
            pltpu.VMEM(level_two.shape, BF16),
            pltpu.VMEM(level_three.shape, BF16),
            pltpu.VMEM((blocks, shards * slots, depth), BF16),
            pltpu.VMEM((blocks, size, shards * slots), F32),
            pltpu.VMEM((shards, blocks * slots, 2 * size), BF16),
            pltpu.VMEM((shards * slots, 128), F32),
            pltpu.VMEM((rows, rows), BF16),
            pltpu.VMEM((shards * slots, 128), F32),
            pltpu.VMEM((shards, 2 * blocks, 128), F32),
            pltpu.VMEM((shards, 2 * blocks, 128), F32),
            pltpu.VMEM((count, all_blocks, rows), BF16),
            pltpu.VMEM((count, rows), F32),
            pltpu.VMEM((shards, blocks, 128), F32),
            pltpu.VMEM((shards, blocks, 128), F32),
            pltpu.VMEM((blocks, shards * slots), F32),
            pltpu.VMEM((blocks, size, depth), F32),
            pltpu.VMEM((2, size, depth), BF16),
            pltpu.VMEM((4, size, depth), BF16),
            pltpu.VMEM((8, size, depth), BF16),
            pltpu.VMEM((4, blocks, 128), F32),
            pltpu.VMEM((blocks, 128), F32),
            pltpu.VMEM((size, 128), F32),
            dma((2,)), dma((2,)), dma((4,)), dma((40,)), dma((40,)), dma((32,)), dma((32,)),
            dma((shards,)), dma((shards,)), dma((shards,)), dma((shards,)), dma((shards,)), dma((shards,)),
            dma((16,)), dma((16,)),
        ],
        compiler_params=pltpu.CompilerParams(
            vmem_limit_bytes=VMEM_LIMIT, collective_id=0, has_side_effects=True
        ),
    )(temper, extended, packed, level_two, level_three)

    soft_codes, candidate_scores = pl.pallas_call(
        spread_kernel,
        in_specs=[
            pl.BlockSpec(memory_space=pltpu.SMEM),
            whole((rows, count)),
            whole((rows, count)),
            whole((all_blocks * slots, 2 * size)),
        ],
        out_shape=[
            jax.ShapeDtypeStruct((rows, count * size), BF16),
            jax.ShapeDtypeStruct((rows, count * size), F32),
        ],
        scratch_shapes=[
            pltpu.VMEM((all_blocks * slots, 2 * size), F32),
            pltpu.VMEM((16, count * size), F32),
            pltpu.VMEM((16, count * size), F32),
        ],
        compiler_params=params(),
    )(place.T.reshape(-1), scale.T, mass.T, returned.reshape(all_blocks * slots, 2 * size))

    new_centroids = sums.reshape(blocks * size, depth).astype(F32)
    return soft_codes, candidate_scores, new_centroids, cluster_mass.reshape(blocks * size)


def solution(mesh):
    rows = P(("dp", "clus"), None)
    return jax.shard_map(
        body,
        mesh=mesh,
        in_specs=(rows, rows, rows, P("clus"), P("clus", None), P("clus", None)),
        out_specs=(rows, rows, P("clus", None), P("clus")),
        check_vma=False,
    )
```

time: 327 us -> 255 us (0.78)
  Pallas kernels: 79.8 us -> 241 us
  waiting for transfers between devices: 134 us -> 0 us
  blocking collectives: 62.4 us -> 0 us
  between operations: 14.2 us -> 0.65 us
  local copies, waits for them, and re-layouts: 17.3 us -> 5.28 us
  starting transfers between devices: 6.12 us -> 0 us
  other arithmetic: 12.1 us -> 6.3 us
    pallas_call x3 -> x1, Pallas kernels: 65.6 us -> 227 us  [body(): pl.pallas_call(fused_kernel, in_specs=[pl.BlockSpec(memory_space=pltpu.SM...]
    all_gather x1 -> x0, waiting for transfers between devices: 75.3 us -> none  [body(): all_rows = lax.all_gather(embeddings, 'clus', axis=0, tiled=True)]
    all_to_all x1 -> x0, waiting for transfers between devices: 36.3 us -> none  [body(): lax.all_to_all(pay, 'clus', split_axis=0, concat_axis=0, tiled=True)]
    all_gather x1 -> x0, blocking collectives: 29.1 us -> none  [body(): all_packed = lax.all_gather(packed, 'clus', axis=0, tiled=False)]
    all_to_all x2 -> x0, blocking collectives: 22.4 us -> none  [the longest x1 11.6 us: body(): kept = lax.all_to_all(kept, 'clus', split_axis=0, concat_axis=0, tiled=True)]
    psum x1 -> x0, waiting for transfers between devices: 21.4 us -> none  [body(): weighted, cluster_mass = lax.psum((partial, partial_mass), 'dp')]
    psum x1 -> x0, blocking collectives: 10.8 us -> none  [body(): weighted, cluster_mass = lax.psum((partial, partial_mass), 'dp')]
    reshape x3 -> x0, local copies, waits for them, and re-layouts: 10.2 us -> none  [the longest x1 6.43 us: body(): level_three.reshape(blocks, kinds * size, depth)]
  transfers between devices with their start and end apart: 3 -> 0, of which waited for: 3 -> 0; matrix products, arithmetic and copies ran while one was open for 5% -> 0% of each run, Pallas kernels for 4% -> 0%
where the time goes in v2:
time: 255 us; the launch traced here: 254 us
  Pallas kernels  241 us (95%)
  other arithmetic  6.3 us (2%)
  local copies, waits for them, and re-layouts  5.28 us (2%)
    pallas_call x1, Pallas kernels, body(): pl.pallas_call(fused_kernel, in_specs=[pl.BlockSpec(memory_space=pltpu.SM...  227 us
    pallas_call x1, Pallas kernels, body(): pl.pallas_call(spread_kernel, in_specs=[pl.BlockSpec(memory_space=pltpu.S...  14.2 us

profile of v2, /device:TPU:8, one launch (start us, length us, event | category | flops | bytes accessed | tf_op | source)
XLA Modules:
  0.0 253.6 jit_solution(2993729530772653824)
XLA Ops:
  0.6 1.4 add_bitcast_fusion
  2.0 2.3 pad_maximum_fusion.ext_ref
  4.3 227.2 %shard_map.93 = (bf16[32,528,1024]{2,1,0:T(8,128)(2,1)}, bf16[32,256,256]{2,1,0:T(8,128)(2,1)}, f32[8,512]{1,0:T(8,128)}, f32[8,512]{1,0:T(8,128)}, s32[8,512]{1...) custom-call(f32[8]{0:T(128)} %temper_ref.1, bf16[528,1024]{1,0:T(8,128)(2,1)} %pad_maximum_fusion.ext_ref, ...), custom_call_target="tpu_custom_call" | custom-call | tf_op jit(solution)/shard_map/pallas_call | solution.py:571
  231.5 0.8 copy.12
  232.4 0.7 reshape.20.slot_ref
  233.1 1.6 copy.13
  234.7 1.5 copy.14
  236.2 0.0 copy-start
  236.2 14.2 %shard_map.94 = (bf16[512,1024]{1,0:T(8,128)(2,1)}, f32[512,1024]{1,0:T(8,128)}) custom-call(s32[4096]{0:T(1024)} %reshape.20.slot_ref, f32[512,8]{1,0:T(8,128)} %bitcast.15, f32[512,8]{1,0:T(8,128)} %bitcast.16, bf16[8192,256]{1,0:T(8,128)(2,1)} %bitcast.14), custom_call_target="tpu_custom_call" | custom-call | tf_op jit(solution)/shard_map/pallas_call | solution.py:617
  250.4 0.0 copy-done
  250.4 0.0 copy-start.1
  250.4 2.6 %bitcast_convert_fusion = f32[1024,1024]{1,0:T(8,128)} fusion(bf16[8,128,1024]{2,1,0:T(8,128)(2,1)S(1)} %copy-done), kind=kLoop, calls=%fused_computation | loop fusion | flops 1048576 | bytes 6291456 | tf_op jit(solution)/shard_map/convert_element_type | solution.py:637
  253.0 0.0 copy-done.1
  253.0 0.6 copy.16
  (1 shorter events, 0.0 us)
Async XLA Ops:
  236.2 14.2 %copy-start = (bf16[8,128,1024]{2,1,0:T(8,128)(2,1)S(1)}, bf16[8,128,1024]{2,1,0:T(8,128)(2,1)}, u32[]{:S(2)}) copy-start(bf16[8,128,1024]{2,1,0:T(8,128)(2,1)} %get-tuple-element.18) | copy-start | bytes 6291460
  250.4 2.6 %copy-start.1 = (f32[8,128]{1,0:T(8,128)S(1)}, f32[8,128]{1,0:T(8,128)}, u32[]{:S(2)}) copy-start(f32[8,128]{1,0:T(8,128)} %get-tuple-element.19) | copy-start | bytes 12292

commit v3 on v2

--- a/solution.py
+++ b/solution.py
@@ -1,3 +1,5 @@
+import functools
+
 import jax
 import jax.numpy as jnp
 from jax import lax
@@ -7,13 +9,14 @@
 
 F32, BF16, I32 = jnp.float32, jnp.bfloat16, jnp.int32
 MESH = pl.DeviceIdType.MESH
-VMEM_LIMIT = 60 << 20
+VMEM_LIMIT = 62 << 20
 
 ORDER = (
-    (0, 0), (1, 0), (3, 0), (0, 1), (0, 3), (2, 0), (0, 2), (1, 1),
-    (3, 3), (3, 1), (1, 3), (2, 1), (2, 3), (1, 2), (3, 2), (2, 2),
+    (0, 0), (1, 0), (3, 0), (0, 1), (0, 3), (1, 1), (1, 3), (3, 1),
+    (3, 3), (2, 0), (0, 2), (2, 1), (1, 2), (2, 3), (3, 2), (2, 2),
 )
 WAVES = (0, 12, 24, 32)
+CUTS = (14, 18, 22, 26)
 RING = (0, 1, 3, 2)
 
 
@@ -44,15 +47,35 @@
     return high, middle, low
 
 
+def prepare_kernel(all_blocks, slots, packed_ref, rows_ref, ext_ref, slot_ref):
+    parents, rows = packed_ref.shape
+    depth = rows_ref.shape[1]
+    named = lax.shift_right_logical(packed_ref[...], 1)
+    kind = packed_ref[...] & 1
+    ids = jnp.concatenate([named.astype(F32), kind.astype(F32)], axis=0).astype(BF16)
+    ext_ref[0:2 * parents, 0:rows] = ids
+    ext_ref[0:2 * parents, rows:depth] = jnp.zeros((2 * parents, depth - rows), BF16)
+    ext_ref[2 * parents:2 * parents + rows, :] = rows_ref[...]
+    number = lax.broadcasted_iota(I32, (all_blocks, rows), 0)
+    hit = jnp.zeros((all_blocks, rows), F32)
+    for j in range(parents):
+        hit = hit + jnp.where(named[j:j + 1] == number, 1.0, 0.0)
+    rank = jnp.dot(hit.astype(BF16), strict_upper(rows), preferred_element_type=F32)
+    for j in range(parents):
+        own = jnp.sum(jnp.where(named[j:j + 1] == number, rank, 0.0), axis=0, keepdims=True)
+        slot_ref[j:j + 1, :] = named[j:j + 1] * slots + own.astype(I32)
+
+
 def fused_kernel(
-    temper_ref, ext_ref, packed_ref, two_ref, three_ref,
-    buf_ref, ret_ref, scale_ref, mass_ref, slot_ref, fin_ref, total_ref,
+    temper_ref, slot_ref, ext_ref, place_ref, two_ref, three_ref,
+    buf_ref, fin_ref, total_ref, codes_ref, deeper_ref,
     rowbuf, w2, w3, g, et, pay, child, upper, stats, stat_out, stat_in, onehot, item_rank, back_out, back_in,
     sc, part, relay_in, near_in, own, mass_all, mass_send, column_scr,
+    ret_ref, wide, scale_mass, code_rows, deep_rows, out_sem,
     load_sem, w_sem, local_sem, ring_send, ring_recv, sib_send, sib_recv, pay_send, pay_recv,
     stat_send, stat_recv, back_send, back_recv, dp_send, dp_recv,
 ):
-    parents, rows = packed_ref.shape
+    parents, rows = place_ref.shape
     total_rows, depth = ext_ref.shape
     slots = 32
     blocks = temper_ref.shape[0]
@@ -161,6 +184,8 @@
         go(ring(half, 3, chip(half, 1, 0), half + "1", first_axis(half, 3)))
         arrival(half, 0, chip(half, 3, 0), half).wait_recv()
         go(ring(half, 2, chip(half, 3, 0), half + "0", first_axis(half, 1)))
+
+    def first_near_on(half):
         enter_second(half, 1)
         enter_second(half, 2)
         share(half, chip(half, 1, 0))
@@ -188,27 +213,39 @@
         share(half, chip(half, o, 2))
 
     def load(p):
-        return pltpu.make_async_copy(buf_ref.at[source(p)], rowbuf.at[p % 2], load_sem.at[p % 2])
+        return pltpu.make_async_copy(buf_ref.at[source(p)], rowbuf.at[p % 4], load_sem.at[p % 4])
 
     first_block = (me * blocks).astype(F32)
 
-    def gather(low, high):
+    def pay_copy(p, index, device):
+        return pltpu.make_async_remote_copy(
+            src_ref=pay.at[p], dst_ref=ret_ref.at[index], send_sem=pay_send.at[p], recv_sem=pay_recv.at[p],
+            device_id=(dp, device), device_id_type=MESH,
+        )
+
+    def start_pay(p):
+        pay_copy(p, me, source(p)).start()
+
+    def gather(low, high, send=None):
         for q in range(low // 2, high // 2):
             shared("A", q)
             shared("B", q)
-        load(low).start()
+        for p in range(low, min(low + 3, high)):
+            load(jnp.int32(p)).start()
         slot_id = lax.broadcasted_iota(I32, (slots, rows), 0).astype(F32)
         lane = lax.broadcasted_iota(I32, (slots, 128), 1)
 
         @pl.loop(low, high)
         def _(p):
             load(p).wait()
-
-            @pl.when(p + 1 < high)
+            if send is not None:
+                start_pay(p + (send - low))
+
+            @pl.when(p + 3 < high)
             def _():
-                load(p + 1).start()
-
-            meta = rowbuf[p % 2, 0:2 * parents, 0:rows].astype(F32)
+                load(p + 3).start()
+
+            meta = rowbuf[p % 4, 0:2 * parents, 0:rows].astype(F32)
             block = meta[:parents] - first_block
             kind = meta[parents:]
             hits, kinds = [], []
@@ -228,7 +265,7 @@
                 selects.append(jnp.where(select, 1.0, 0.0).astype(BF16))
             select = jnp.concatenate(selects, axis=0)
             picked = jnp.dot(
-                select, rowbuf[p % 2, ids:total_rows, :], preferred_element_type=F32
+                select, rowbuf[p % 4, ids:total_rows, :], preferred_element_type=F32
             ).astype(BF16)
             place = pl.ds(pl.multiple_of(p * slots, slots), slots)
             child[place, :] = child_lanes
@@ -237,13 +274,18 @@
 
     contract_last = (((1,), (1,)), ((), ()))
 
-    def score(wave, low, high):
+    def score(wave, low, high, send=None):
         start, count = WAVES[wave] * slots, (WAVES[wave + 1] - WAVES[wave]) * slots
         here = slice(start, start + count)
         lane = lax.broadcasted_iota(I32, (count, 128), 1)
 
         @pl.loop(low, high)
         def _(b):
+            if send is not None:
+                @pl.when(b % 2 == 0)
+                def _():
+                    start_pay(b // 2 + send)
+
             x = g[b, here, :]
             near = lax.dot_general(
                 x, w2[pl.ds(pl.multiple_of(b * size, size), size), :], contract_last, preferred_element_type=F32
@@ -289,14 +331,8 @@
             stat_in[me] = stat_out[0]
         each(low, high, lambda p: stat_copy(p, me, source(p)).start())
 
-    def pay_copy(p, index, device):
-        return pltpu.make_async_remote_copy(
-            src_ref=pay.at[p], dst_ref=ret_ref.at[index], send_sem=pay_send.at[p], recv_sem=pay_recv.at[p],
-            device_id=(dp, device), device_id_type=MESH,
-        )
-
     def send_pay(low, high):
-        each(low, high, lambda p: pay_copy(p, me, source(p)).start())
+        each(low, high, start_pay)
 
     def back_copy(p, index, device):
         return pltpu.make_async_remote_copy(
@@ -324,56 +360,51 @@
     own_out = pltpu.make_async_copy(rowbuf.at[0], buf_ref.at[me], local_sem.at[1])
     own_out.start()
 
-    named = lax.shift_right_logical(packed_ref[...], 1)
+    named = lax.shift_right_logical(place_ref[...], 5)
+    item_rank[...] = (place_ref[...] & (slots - 1)).astype(F32)
     number = lax.broadcasted_iota(I32, (all_blocks, rows), 0)
-    hit = jnp.zeros((all_blocks, rows), F32)
     for j in range(parents):
-        one = jnp.where(named[j:j + 1] == number, 1.0, 0.0)
-        hit = hit + one
-        onehot[j] = one.astype(BF16)
-    own_rank = jnp.dot(hit.astype(BF16), upper[...], preferred_element_type=F32)
-    for j in range(parents):
-        item_rank[j:j + 1, :] = jnp.sum(onehot[j].astype(F32) * own_rank, axis=0, keepdims=True)
-    slot_ref[...] = named * slots + item_rank[...].astype(I32)
+        onehot[j] = jnp.where(named[j:j + 1] == number, 1.0, 0.0).astype(BF16)
     own_out.wait()
 
     first_near("A")
     first_near("B")
+    first_near_on("A")
+    first_near_on("B")
     gather(0, 2)
     second_near("A", 0)
     second_near("B", 0)
     first_far("A")
     first_far("B")
-    gather(2, 6)
+    gather(2, 10)
+    second_near("A", 1)
+    second_near("B", 1)
+    gather(10, 12)
+    in_two.wait()
+    in_three.wait()
+    score(0, 0, blocks)
+    second_near("A", 2)
+    second_near("B", 2)
+    send_stats(0)
+    gather(12, 18)
     second_far("A", 0)
     second_far("B", 0)
-    second_near("A", 1)
-    second_near("B", 1)
-    gather(6, 12)
-    in_two.wait()
-    in_three.wait()
-    second_near("A", 2)
-    second_near("B", 2)
-    score(0, 0, blocks)
-    second_far("A", 1)
-    second_far("B", 1)
-    send_stats(0)
-    gather(12, 18)
-    second_far("A", 2)
-    second_far("B", 2)
     gather(18, 22)
     second_near("A", 3)
     second_near("B", 3)
-    gather(22, 24)
+    second_far("A", 1)
+    second_far("B", 1)
+    gather(22, 26)
     score(1, 0, blocks)
-    send_stats(1)
+    second_far("A", 2)
+    second_far("B", 2)
     second_far("A", 3)
     second_far("B", 3)
-    send_pay(0, PAY_CUTS[0])
-    gather(24, 32)
-    score(2, 0, blocks)
+    send_stats(1)
+    gather(26, 32, 1)
+    score(2, 0, blocks, 7)
     send_stats(2)
-    send_pay(PAY_CUTS[0], PAY_CUTS[1])
+    send_pay(11, CUTS[0])
     own_pay = pltpu.make_async_copy(pay.at[0], ret_ref.at[me], local_sem.at[0])
     own_pay.start()
 
@@ -394,8 +425,8 @@
     amount = jnp.concatenate(amounts, axis=0)
     weight = jnp.exp(most - jnp.max(most, axis=0, keepdims=True))
     scale = weight / jnp.sum(weight * amount, axis=0, keepdims=True)
-    scale_ref[...] = scale
-    mass_ref[...] = scale * amount
+    blank = jnp.zeros((128 - 2 * parents, rows), F32)
+    scale_mass[...] = jnp.concatenate([scale, scale * amount * parents, blank], axis=0).T
     back = jnp.zeros((all_blocks, 4 * slots), F32)
     for j in range(parents):
         pick = slot_row == item_rank[j:j + 1, :]
@@ -408,7 +439,7 @@
         back_out[o] = back[o * blocks:(o + 1) * blocks, :]
     back_in[0] = back_out[me]
     each(0, shards, lambda p: back_copy(p, holder(p), holder(p)).start())
-    send_pay(PAY_CUTS[1], shards)
+    send_pay(CUTS[0], CUTS[1])
     each(0, shards, lambda p: back_copy(p, holder(p), holder(p)).wait_recv())
     lane8 = lax.broadcasted_iota(I32, (blocks, 128), 1)
     for t in range(shards // 4):
@@ -427,12 +458,35 @@
     lane128 = lax.broadcasted_iota(I32, (size, 128), 1)
     column_scr[...] = jnp.zeros_like(column_scr)
 
-    @pl.loop(0, blocks)
-    def _(i):
-        b = (2 * ((dp + 2) % 4) + i) % blocks
-        value, column = sums(b)
-        part[b] = value
-        column_scr[...] = jnp.where(lane128 == b, column, column_scr[...])
+    def sum_blocks(first, low, high):
+        @pl.loop(low, high)
+        def _(i):
+            b = (2 * first + i) % blocks
+            value, column = sums(b)
+            part[b] = value
+            column_scr[...] = jnp.where(lane128 == b, column, column_scr[...])
+
+    def widen(low, high):
+        @pl.loop(low, high)
+        def _(o):
+            here = pl.ds(pl.multiple_of(o * blocks * slots, blocks * slots), blocks * slots)
+            wide[here, :] = ret_ref[o].astype(F32)
+
+    def spread_rows(low, high):
+        @pl.loop(low, high)
+        def _(i):
+            for r in range(16):
+                for j in range(parents):
+                    item = wide[pl.ds(slot_ref[j, i * 16 + r], 1), :]
+                    code_rows[r:r + 1, j * size:(j + 1) * size] = item[:, :size]
+                    deep_rows[r:r + 1, j * size:(j + 1) * size] = item[:, size:]
+            here = pl.ds(pl.multiple_of(i * 16, 16), 16)
+            low_rows = pl.ds(pl.multiple_of((i % 8) * 16, 16), 16)
+            factors = scale_mass[here, :]
+            for j in range(parents):
+                part_j = slice(j * size, (j + 1) * size)
+                g[0, here, part_j] = (code_rows[:, part_j] * factors[:, j:j + 1]).astype(BF16)
+                part[i // 8, low_rows, part_j] = deep_rows[:, part_j] * factors[:, parents + j:parents + j + 1]
 
     def dp_copy(index, source_ref, target_ref, step):
         return pltpu.make_async_remote_copy(
@@ -441,31 +495,37 @@
         )
 
     right, left, across = (dp + 1) % 4, (dp + 3) % 4, (dp + 2) % 4
+    sum_blocks(across, 0, 2)
+    own[0] = part[2 * across].astype(BF16)
+    own[1] = part[2 * across + 1].astype(BF16)
+    relay = [dp_copy(0, own.at[0], relay_in.at[0], 1), dp_copy(1, own.at[1], relay_in.at[1], 3)]
+    for copy in relay:
+        copy.start()
+    send_pay(CUTS[1], CUTS[2])
+    sum_blocks(across, 2, 4)
+    sum_blocks(across, 6, 8)
+    own[3] = part[2 * right + 1].astype(BF16)
+    own[4] = part[2 * left].astype(BF16)
+    near = [
+        dp_copy(2, own.at[2], near_in.at[0], 1), dp_copy(3, own.at[3], near_in.at[1], 1),
+        dp_copy(4, own.at[4], near_in.at[2], 3), dp_copy(5, own.at[5], near_in.at[3], 3),
+    ]
+    near[1].start()
+    near[2].start()
+    send_pay(CUTS[2], CUTS[3])
+    sum_blocks(across, 4, 6)
     mass_send[...] = column_scr[...].T[0:blocks, :]
     mass_all[dp] = mass_send[...]
     mass_copies = [dp_copy(8 + d, mass_send, mass_all.at[dp], d) for d in (1, 2, 3)]
     for copy in mass_copies:
         copy.start()
-    half_part = near_in
-    own[0] = part[2 * across].astype(BF16)
-    own[1] = part[2 * across + 1].astype(BF16)
-    relay = [dp_copy(0, own.at[0], relay_in.at[0], 1), dp_copy(1, own.at[1], relay_in.at[1], 3)]
-    for copy in relay:
-        copy.start()
-    own[3] = part[2 * right + 1].astype(BF16)
-    own[4] = part[2 * left].astype(BF16)
-    near = [
-        dp_copy(2, own.at[2], half_part.at[0], 1), dp_copy(3, own.at[3], half_part.at[1], 1),
-        dp_copy(4, own.at[4], half_part.at[2], 3), dp_copy(5, own.at[5], half_part.at[3], 3),
-    ]
-    near[1].start()
-    near[2].start()
     relay[0].wait_recv()
     own[2] = (part[2 * right] + relay_in[0].astype(F32)).astype(BF16)
     near[0].start()
     relay[1].wait_recv()
     own[5] = (part[2 * left + 1] + relay_in[1].astype(F32)).astype(BF16)
     near[3].start()
+    send_pay(CUTS[3], shards)
     for copy in mass_copies:
         copy.wait_recv()
     all_mass = ((mass_all[0] + mass_all[1]) + mass_all[2]) + mass_all[3]
@@ -477,7 +537,7 @@
     for i in range(2):
         b = 2 * dp + i
         column = jnp.sum(jnp.where(lane128 == b, column_scr[...], 0.0), axis=1, keepdims=True)
-        value = part[b] + (half_part[i].astype(F32) + half_part[2 + i].astype(F32))
+        value = part[b] + (near_in[i].astype(F32) + near_in[2 + i].astype(F32))
         own[6 + i] = (value / column).astype(BF16)
     ready = [
         dp_copy(12, own.at[6], fin_ref.at[2 * dp], 1), dp_copy(13, own.at[7], fin_ref.at[2 * dp + 1], 3),
@@ -488,64 +548,38 @@
     own_fin = [pltpu.make_async_copy(own.at[6 + i], fin_ref.at[2 * dp + i], local_sem.at[2 + i]) for i in range(2)]
     for copy in own_fin:
         copy.start()
+    each(0, shards, lambda p: pay_copy(p, holder(p), source(p)).wait_recv())
+    own_pay.wait()
+    widen(0, shards)
     dp_copy(12, own.at[6], fin_ref.at[2 * left], 1).wait_recv()
     onward = [dp_copy(6, fin_ref.at[2 * left], fin_ref.at[2 * left], 1)]
     onward[0].start()
     dp_copy(13, own.at[7], fin_ref.at[2 * right + 1], 3).wait_recv()
     onward.append(dp_copy(7, fin_ref.at[2 * right + 1], fin_ref.at[2 * right + 1], 3))
     onward[1].start()
+    steps = rows // 16
+    spread_rows(0, steps)
+    outs = [pltpu.make_async_copy(g.at[0, pl.ds(0, rows), :], codes_ref, out_sem.at[4])]
+    for i in range(rows // size):
+        outs.append(pltpu.make_async_copy(part.at[i], deeper_ref.at[pl.ds(i * size, size), :], out_sem.at[i]))
+    for copy in outs:
+        copy.start()
     dp_copy(14, own.at[7], fin_ref.at[2 * left + 1], 1).wait_recv()
     dp_copy(15, own.at[6], fin_ref.at[2 * right], 3).wait_recv()
     dp_copy(6, own.at[6], fin_ref.at[2 * across], 1).wait_recv()
     dp_copy(7, own.at[7], fin_ref.at[2 * across + 1], 3).wait_recv()
 
-    each(0, shards, lambda p: pay_copy(p, holder(p), source(p)).wait_recv())
     for copy in sent + mass_copies + relay + near + ready + onward:
         copy.wait_send()
     each(0, shards, lambda p: pay_copy(p, me, source(p)).wait_send())
     each(0, shards, lambda p: stat_copy(p, me, source(p)).wait_send())
     each(0, shards, lambda p: back_copy(p, holder(p), holder(p)).wait_send())
-    own_pay.wait()
-    for copy in own_fin:
+    for copy in own_fin + outs:
         copy.wait()
-
-
-PAY_CUTS = (8, 16)
-
-
-def spread_kernel(slot_ref, scale_ref, mass_ref, pay_ref, codes_ref, deeper_ref, wide_ref, code_ref, deep_ref):
-    rows, parents = scale_ref.shape
-    size = pay_ref.shape[1] // 2
-    count = pay_ref.shape[0]
-    chunk = min(512, count)
-
-    @pl.loop(0, count // chunk)
-    def _(i):
-        here = pl.ds(pl.multiple_of(i * chunk, chunk), chunk)
-        wide_ref[here, :] = pay_ref[here, :].astype(F32)
-
-    @pl.loop(0, rows // 16)
-    def _(i):
-        for r in range(16):
-            for j in range(parents):
-                slot = slot_ref[(i * 16 + r) * parents + j]
-                item = wide_ref[pl.ds(slot, 1), :]
-                code_ref[r:r + 1, j * size:(j + 1) * size] = item[:, :size]
-                deep_ref[r:r + 1, j * size:(j + 1) * size] = item[:, size:]
-        here = pl.ds(pl.multiple_of(i * 16, 16), 16)
-        scale, mass = scale_ref[here, :], mass_ref[here, :]
-        for j in range(parents):
-            part = slice(j * size, (j + 1) * size)
-            codes_ref[here, part] = (code_ref[:, part] * scale[:, j:j + 1]).astype(BF16)
-            deeper_ref[here, part] = deep_ref[:, part] * (parents * mass[:, j:j + 1])
 
 
 def params():
     return pltpu.CompilerParams(vmem_limit_bytes=VMEM_LIMIT)
-
-
-def whole(shape):
-    return pl.BlockSpec(shape, lambda *_: (0,) * len(shape))
 
 
 def body(embeddings, parents, children, temper, level_two, level_three):
@@ -560,29 +594,32 @@
     assert kinds == 2 and shards == 32 and slots == 32 and blocks == 8 and lax.axis_size("dp") == 4
 
     packed = (parents * kinds + children).T
-    ids = jnp.concatenate([parents.T, children.T], axis=0).astype(BF16)
-    ids = jnp.pad(ids, ((0, 0), (0, depth - rows)))
-    extended = jnp.concatenate([ids, embeddings], axis=0)
-    total_rows = extended.shape[0]
+    total_rows = rows + 2 * count
+    extended, place = pl.pallas_call(
+        functools.partial(prepare_kernel, all_blocks, slots),
+        out_shape=[jax.ShapeDtypeStruct((total_rows, depth), BF16), jax.ShapeDtypeStruct((count, rows), I32)],
+        compiler_params=params(),
+    )(packed, embeddings)
     anywhere = pl.BlockSpec(memory_space=pl.ANY)
     vmem = pl.BlockSpec(memory_space=pltpu.VMEM)
     dma = pltpu.SemaphoreType.DMA
 
-    _, returned, scale, mass, place, sums, cluster_mass = pl.pallas_call(
+    _, sums, cluster_mass, soft_codes, candidate_scores = pl.pallas_call(
         fused_kernel,
-        in_specs=[pl.BlockSpec(memory_space=pltpu.SMEM), anywhere, vmem, anywhere, anywhere],
-        out_specs=[anywhere, anywhere, vmem, vmem, vmem, anywhere, vmem],
+        in_specs=[
+            pl.BlockSpec(memory_space=pltpu.SMEM), pl.BlockSpec(memory_space=pltpu.SMEM),
+            anywhere, vmem, anywhere, anywhere,
+        ],
+        out_specs=[anywhere, anywhere, vmem, anywhere, anywhere],
         out_shape=[
             jax.ShapeDtypeStruct((shards, total_rows, depth), BF16),
-            jax.ShapeDtypeStruct((shards, blocks * slots, 2 * size), BF16),
-            jax.ShapeDtypeStruct((count, rows), F32),
-            jax.ShapeDtypeStruct((count, rows), F32),
-            jax.ShapeDtypeStruct((count, rows), I32),
             jax.ShapeDtypeStruct((blocks, size, depth), BF16),
             jax.ShapeDtypeStruct((blocks, size), F32),
+            jax.ShapeDtypeStruct((rows, count * size), BF16),
+            jax.ShapeDtypeStruct((rows, count * size), F32),
         ],
         scratch_shapes=[
-            pltpu.VMEM((2, total_rows, depth), BF16),
+            pltpu.VMEM((4, total_rows, depth), BF16),
             pltpu.VMEM(level_two.shape, BF16),
             pltpu.VMEM(level_three.shape, BF16),
             pltpu.VMEM((blocks, shards * slots, depth), BF16),
@@ -605,34 +642,20 @@
             pltpu.VMEM((4, blocks, 128), F32),
             pltpu.VMEM((blocks, 128), F32),
             pltpu.VMEM((size, 128), F32),
-            dma((2,)), dma((2,)), dma((4,)), dma((40,)), dma((40,)), dma((32,)), dma((32,)),
+            pltpu.VMEM((shards, blocks * slots, 2 * size), BF16),
+            pltpu.VMEM((shards * blocks * slots, 2 * size), F32),
+            pltpu.VMEM((rows, 128), F32),
+            pltpu.VMEM((16, count * size), F32),
+            pltpu.VMEM((16, count * size), F32),
+            dma((5,)),
+            dma((4,)), dma((2,)), dma((4,)), dma((40,)), dma((40,)), dma((32,)), dma((32,)),
             dma((shards,)), dma((shards,)), dma((shards,)), dma((shards,)), dma((shards,)), dma((shards,)),
             dma((16,)), dma((16,)),
         ],
         compiler_params=pltpu.CompilerParams(
             vmem_limit_bytes=VMEM_LIMIT, collective_id=0, has_side_effects=True
         ),
-    )(temper, extended, packed, level_two, level_three)
-
-    soft_codes, candidate_scores = pl.pallas_call(
-        spread_kernel,
-        in_specs=[
-            pl.BlockSpec(memory_space=pltpu.SMEM),
-            whole((rows, count)),
-            whole((rows, count)),
-            whole((all_blocks * slots, 2 * size)),
-        ],
-        out_shape=[
-            jax.ShapeDtypeStruct((rows, count * size), BF16),
-            jax.ShapeDtypeStruct((rows, count * size), F32),
-        ],
-        scratch_shapes=[
-            pltpu.VMEM((all_blocks * slots, 2 * size), F32),
-            pltpu.VMEM((16, count * size), F32),
-            pltpu.VMEM((16, count * size), F32),
-        ],
-        compiler_params=params(),
-    )(place.T.reshape(-1), scale.T, mass.T, returned.reshape(all_blocks * slots, 2 * size))
+    )(temper, place, extended, place, level_two, level_three)
 
     new_centroids = sums.reshape(blocks * size, depth).astype(F32)
     return soft_codes, candidate_scores, new_centroids, cluster_mass.reshape(blocks * size)

time: 255 us -> 213 us (0.84)
  Pallas kernels: 241 us -> 201 us
    pallas_call x1, Pallas kernels: 227 us -> 197 us  [body(): pl.pallas_call(fused_kernel, in_specs=[pl.BlockSpec(memory_space=pltpu.SM...]
    pallas_call x1, Pallas kernels: 14.2 us -> 3.47 us  [body(): pl.pallas_call(functools.partial(prepare_kernel, all_blocks, slots), out_...]
    unnamed x5 -> x9, local copies, waits for them, and re-layouts: 0.6 us -> 3.89 us
    pallas_call x2 -> x0, local copies, waits for them, and re-layouts: 3.09 us -> none  [body(): pl.pallas_call(fused_kernel, in_specs=[pl.BlockSpec(memory_space=pltpu.SM...]
where the time goes in v3:
time: 213 us; the launch traced here: 211 us
  Pallas kernels  201 us (94%)
  other arithmetic  5.5 us (3%)
  local copies, waits for them, and re-layouts  3.89 us (2%)
    pallas_call x1, Pallas kernels, body(): pl.pallas_call(fused_kernel, in_specs=[pl.BlockSpec(memory_space=pltpu.SM...  197 us

profile of v3, /device:TPU:8, one launch (start us, length us, event | category | flops | bytes accessed | tf_op | source)
XLA Modules:
  0.0 211.0 jit_solution(2720966425982403726)
XLA Ops:
  0.6 1.3 add_bitcast_fusion.packed_ref
  2.0 3.5 %shard_map.93 = (bf16[528,1024]{1,0:T(8,128)(2,1)}, s32[8,512]{1,0:T(8,128)}) custom-call(s32[8,512]{1,0:T(8,128)} %add_bitcast_fusion.packed_ref, bf16[512,1024]{1,0:T(8,128)(2,1)} %rows_ref.1), custom_call_target="tpu_custom_call" | custom-call | tf_op jit(solution)/shard_map/pallas_call | solution.py:598
  5.4 197.5 %shard_map.94 = (bf16[32,528,1024]{2,1,0:T(8,128)(2,1)}, bf16[8,128,1024]{2,1,0:T(8,128)(2,1)}, f32[8,128]{1,0:T(8,128)}, bf16[512,1024]{1,0:T(8,128)(2,1)}, f32[512,1024]{1,0:T(8,128)}) custom-call(f32[8]{0:T(128)} %temper_ref.1, s32[8,512]{1,0:T(8,128)} %get-tuple-element.10.slot_ref.place_ref, bf16[528,1024]{1,0:T(8,128)(2,1)} %get-tuple-element.11.ext_ref, ...), custom_call_target="tpu_custom_call" | custom-call | tf_op jit(solution)/shard_map/pallas_call | solution.py:607
  202.9 0.0 copy-start.1
  202.9 4.2 %bitcast_convert_fusion = f32[1024,1024]{1,0:T(8,128)} fusion(bf16[8,128,1024]{2,1,0:T(8,128)(2,1)} %get-tuple-element.14), kind=kLoop, calls=%fused_computation | loop fusion | flops 1048576 | bytes 6291456 | tf_op jit(solution)/shard_map/convert_element_type | solution.py:660
  207.1 0.0 copy-done.1
  207.1 0.0 copy-start
  207.1 1.0 copy.13
  208.1 1.0 copy-done
  209.1 0.0 copy-start.2
  209.1 1.3 copy.14
  210.4 0.0 copy-done.2
  210.4 0.6 copy.15
Async XLA Ops:
  202.9 4.2 %copy-start.1 = (bf16[512,1024]{1,0:T(8,128)(2,1)S(1)}, bf16[512,1024]{1,0:T(8,128)(2,1)}, u32[]{:S(2)}) copy-start(bf16[512,1024]{1,0:T(8,128)(2,1)} %get-tuple-element.20) | copy-start | bytes 3145732
  207.1 2.0 copy-start
  209.1 1.3 copy-start.2

commit v4 on v3

--- a/solution.py
+++ b/solution.py
@@ -12,7 +12,7 @@
 VMEM_LIMIT = 62 << 20
 
 ORDER = (
-    (0, 0), (1, 0), (3, 0), (0, 1), (0, 3), (1, 1), (1, 3), (3, 1),
+    (0, 0), (1, 0), (0, 1), (3, 0), (0, 3), (1, 1), (1, 3), (3, 1),
     (3, 3), (2, 0), (0, 2), (2, 1), (1, 2), (2, 3), (3, 2), (2, 2),
 )
 WAVES = (0, 12, 24, 32)
@@ -223,7 +223,8 @@
             device_id=(dp, device), device_id_type=MESH,
         )
 
-    def start_pay(p):
+    def start_pay(k):
+        p = (k // 8) * 8 + (k % 4) * 2 + (k % 8) // 4
         pay_copy(p, me, source(p)).start()
 
     def gather(low, high, send=None):
@@ -548,15 +549,15 @@
     own_fin = [pltpu.make_async_copy(own.at[6 + i], fin_ref.at[2 * dp + i], local_sem.at[2 + i]) for i in range(2)]
     for copy in own_fin:
         copy.start()
-    each(0, shards, lambda p: pay_copy(p, holder(p), source(p)).wait_recv())
-    own_pay.wait()
-    widen(0, shards)
     dp_copy(12, own.at[6], fin_ref.at[2 * left], 1).wait_recv()
     onward = [dp_copy(6, fin_ref.at[2 * left], fin_ref.at[2 * left], 1)]
     onward[0].start()
     dp_copy(13, own.at[7], fin_ref.at[2 * right + 1], 3).wait_recv()
     onward.append(dp_copy(7, fin_ref.at[2 * right + 1], fin_ref.at[2 * right + 1], 3))
     onward[1].start()
+    each(0, shards, lambda p: pay_copy(p, holder(p), source(p)).wait_recv())
+    own_pay.wait()
+    widen(0, shards)
     steps = rows // 16
     spread_rows(0, steps)
     outs = [pltpu.make_async_copy(g.at[0, pl.ds(0, rows), :], codes_ref, out_sem.at[4])]

time: 213 us -> 206 us (0.967)
  Pallas kernels: 201 us -> 195 us
    pallas_call x1, Pallas kernels: 197 us -> 191 us  [body(): pl.pallas_call(fused_kernel, in_specs=[pl.BlockSpec(memory_space=pltpu.SM...]
where the time goes in v4:
time: 206 us; the launch traced here: 205 us
  Pallas kernels  195 us (95%)
  other arithmetic  5.5 us (3%)
  local copies, waits for them, and re-layouts  3.89 us (2%)
    pallas_call x1, Pallas kernels, body(): pl.pallas_call(fused_kernel, in_specs=[pl.BlockSpec(memory_space=pltpu.SM...  191 us
    convert_element_type x1, other arithmetic, body(): new_centroids = sums.reshape(blocks * size, depth).astype(F32)  4.16 us

profile of v4, /device:TPU:8, one launch (start us, length us, event | category | flops | bytes accessed | tf_op | source)
XLA Modules:
  0.0 205.0 jit_solution(5380945854248689607)
XLA Ops:
  0.6 1.3 add_bitcast_fusion.packed_ref
  2.0 3.5 %shard_map.93 = (bf16[528,1024]{1,0:T(8,128)(2,1)}, s32[8,512]{1,0:T(8,128)}) custom-call(s32[8,512]{1,0:T(8,128)} %add_bitcast_fusion.packed_ref, bf16[512,1024]{1,0:T(8,128)(2,1)} %rows_ref.1), custom_call_target="tpu_custom_call" | custom-call | tf_op jit(solution)/shard_map/pallas_call | solution.py:599
  5.4 191.5 %shard_map.94 = (bf16[32,528,1024]{2,1,0:T(8,128)(2,1)}, bf16[8,128,1024]{2,1,0:T(8,128)(2,1)}, f32[8,128]{1,0:T(8,128)}, bf16[512,1024]{1,0:T(8,128)(2,1)}, f32[512,1024]{1,0:T(8,128)}) custom-call(f32[8]{0:T(128)} %temper_ref.1, s32[8,512]{1,0:T(8,128)} %get-tuple-element.10.slot_ref.place_ref, bf16[528,1024]{1,0:T(8,128)(2,1)} %get-tuple-element.11.ext_ref, ...), custom_call_target="tpu_custom_call" | custom-call | tf_op jit(solution)/shard_map/pallas_call | solution.py:608
  196.9 0.0 copy-start.1
  196.9 4.2 %bitcast_convert_fusion = f32[1024,1024]{1,0:T(8,128)} fusion(bf16[8,128,1024]{2,1,0:T(8,128)(2,1)} %get-tuple-element.14), kind=kLoop, calls=%fused_computation | loop fusion | flops 1048576 | bytes 6291456 | tf_op jit(solution)/shard_map/convert_element_type | solution.py:661
  201.1 0.0 copy-done.1
  201.1 0.0 copy-start
  201.1 1.0 copy.13
  202.1 1.0 copy-done
  203.1 0.0 copy-start.2
  203.1 1.3 copy.14
  204.4 0.0 copy-done.2
  204.4 0.6 copy.15
Async XLA Ops:
  196.9 4.2 %copy-start.1 = (bf16[512,1024]{1,0:T(8,128)(2,1)S(1)}, bf16[512,1024]{1,0:T(8,128)(2,1)}, u32[]{:S(2)}) copy-start(bf16[512,1024]{1,0:T(8,128)(2,1)} %get-tuple-element.20) | copy-start | bytes 3145732
  201.1 2.0 copy-start
  203.1 1.3 copy-start.2

commit v5 on v4

--- a/solution.py
+++ b/solution.py
@@ -16,7 +16,7 @@
     (3, 3), (2, 0), (0, 2), (2, 1), (1, 2), (2, 3), (3, 2), (2, 2),
 )
 WAVES = (0, 12, 24, 32)
-CUTS = (14, 18, 22, 26)
+CUTS = (18, 22, 26, 30)
 RING = (0, 1, 3, 2)
 
 
@@ -223,8 +223,11 @@
             device_id=(dp, device), device_id_type=MESH,
         )
 
+    def place_of(k):
+        return (k // 8) * 8 + (k % 4) * 2 + (k % 8) // 4
+
     def start_pay(k):
-        p = (k // 8) * 8 + (k % 4) * 2 + (k % 8) // 4
+        p = place_of(k)
         pay_copy(p, me, source(p)).start()
 
     def gather(low, high, send=None):
@@ -395,17 +398,17 @@
     second_near("B", 3)
     second_far("A", 1)
     second_far("B", 1)
-    gather(22, 26)
+    gather(22, 26, 1)
     score(1, 0, blocks)
     second_far("A", 2)
     second_far("B", 2)
     second_far("A", 3)
     second_far("B", 3)
     send_stats(1)
-    gather(26, 32, 1)
-    score(2, 0, blocks, 7)
+    gather(26, 32, 5)
+    score(2, 0, blocks, 11)
     send_stats(2)
-    send_pay(11, CUTS[0])
+    send_pay(15, CUTS[0])
     own_pay = pltpu.make_async_copy(pay.at[0], ret_ref.at[me], local_sem.at[0])
     own_pay.start()
 
@@ -467,10 +470,17 @@
             part[b] = value
             column_scr[...] = jnp.where(lane128 == b, column, column_scr[...])
 
-    def widen(low, high):
-        @pl.loop(low, high)
-        def _(o):
-            here = pl.ds(pl.multiple_of(o * blocks * slots, blocks * slots), blocks * slots)
+    def widen_arrived():
+        @pl.loop(0, shards)
+        def _(k):
+            p = place_of(k)
+
+            @pl.when(k > 0)
+            def _():
+                pay_copy(p, holder(p), source(p)).wait_recv()
+
+            o = holder(p)
+            here = pl.ds(pl.multiple_of(o * (blocks * slots), blocks * slots), blocks * slots)
             wide[here, :] = ret_ref[o].astype(F32)
 
     def spread_rows(low, high):
@@ -555,9 +565,8 @@
     dp_copy(13, own.at[7], fin_ref.at[2 * right + 1], 3).wait_recv()
     onward.append(dp_copy(7, fin_ref.at[2 * right + 1], fin_ref.at[2 * right + 1], 3))
     onward[1].start()
-    each(0, shards, lambda p: pay_copy(p, holder(p), source(p)).wait_recv())
     own_pay.wait()
-    widen(0, shards)
+    widen_arrived()
     steps = rows // 16
     spread_rows(0, steps)
     outs = [pltpu.make_async_copy(g.at[0, pl.ds(0, rows), :], codes_ref, out_sem.at[4])]

time: 206 us -> 203 us (0.985)
  the two profiles are of different devices: /device:TPU:8 before, /device:TPU:0 now
where the time goes in v5:
time: 203 us
  Pallas kernels  193 us (95%)
  other arithmetic  5.5 us (3%)
  local copies, waits for them, and re-layouts  3.89 us (2%)
    pallas_call x1, Pallas kernels, body(): pl.pallas_call(fused_kernel, in_specs=[pl.BlockSpec(memory_space=pltpu.SM...  190 us
    convert_element_type x1, other arithmetic, body(): new_centroids = sums.reshape(blocks * size, depth).astype(F32)  4.16 us

profile of v5, /device:TPU:0, one launch (start us, length us, event | category | flops | bytes accessed | tf_op | source)
XLA Modules:
  0.0 203.0 jit_solution(17811646841730754986)
XLA Ops:
  0.6 1.3 add_bitcast_fusion.packed_ref
  2.0 3.5 %shard_map.93 = (bf16[528,1024]{1,0:T(8,128)(2,1)}, s32[8,512]{1,0:T(8,128)}) custom-call(s32[8,512]{1,0:T(8,128)} %add_bitcast_fusion.packed_ref, bf16[512,1024]{1,0:T(8,128)(2,1)} %rows_ref.1), custom_call_target="tpu_custom_call" | custom-call | tf_op jit(solution)/shard_map/pallas_call | solution.py:608
  5.4 189.5 %shard_map.94 = (bf16[32,528,1024]{2,1,0:T(8,128)(2,1)}, bf16[8,128,1024]{2,1,0:T(8,128)(2,1)}, f32[8,128]{1,0:T(8,128)}, bf16[512,1024]{1,0:T(8,128)(2,1)}, f32[512,1024]{1,0:T(8,128)}) custom-call(f32[8]{0:T(128)} %temper_ref.1, s32[8,512]{1,0:T(8,128)} %get-tuple-element.10.slot_ref.place_ref, bf16[528,1024]{1,0:T(8,128)(2,1)} %get-tuple-element.11.ext_ref, ...), custom_call_target="tpu_custom_call" | custom-call | tf_op jit(solution)/shard_map/pallas_call | solution.py:617
  195.0 0.0 copy-start.1
  195.0 4.2 %bitcast_convert_fusion = f32[1024,1024]{1,0:T(8,128)} fusion(bf16[8,128,1024]{2,1,0:T(8,128)(2,1)} %get-tuple-element.14), kind=kLoop, calls=%fused_computation | loop fusion | flops 1048576 | bytes 6291456 | tf_op jit(solution)/shard_map/convert_element_type | solution.py:670
  199.1 0.0 copy-done.1
  199.1 0.0 copy-start
  199.1 1.0 copy.13
  200.1 1.0 copy-done
  201.1 0.0 copy-start.2
  201.1 1.3 copy.14
  202.4 0.0 copy-done.2
  202.4 0.6 copy.15
Async XLA Ops:
  195.0 4.2 %copy-start.1 = (bf16[512,1024]{1,0:T(8,128)(2,1)S(1)}, bf16[512,1024]{1,0:T(8,128)(2,1)}, u32[]{:S(2)}) copy-start(bf16[512,1024]{1,0:T(8,128)(2,1)} %get-tuple-element.20) | copy-start | bytes 3145732
  199.1 2.0 copy-start
  201.1 1.3 copy-start.2
